TPU v7x, 128 devices: a whole 4x4x4 slice. The times are simulated.
128 devices in a mesh: tm: 8 (over z, core), space: 16 (over y, x).
Axes of the slice: x: 4, y: 4, z: 4, core: 2. Of those that a mesh axis runs over, the one named last changes fastest.
Arguments:
- noise: bfloat16 [32, 1024, 8192], P('tm', 'space'), may hold values from -4 to 4
- scale: float32 [32, 8192], P('tm'), may hold values from 0.55 to 1
- tiles: bfloat16 [32, 64, 3, 128, 128], P('tm', 'space'), may hold values from -0.375 to 0.375
- columns: int32 [32, 64, 3], P('tm', 'space'), may hold values from 0 to 63, as said below
Outputs:
- samples: bfloat16 [32, 1024, 8192], P('tm', 'space')
Inputs may be any that keep to these rules, and one draw needn't show every extreme that they name: `columns`: in every tile row r of a time step the 3 entries are different, and the first is r itself.
All inputs are finite; a program needn't handle non-finite values.
Results may differ from a plain program's by a relative error of at most 0.03.
Values may be sent and summed in bfloat16 or wider, within the bound.
No kernel may reach another device: no remote copies, remote signals or barrier semaphores. Data moves between devices by JAX's collectives and lax.ppermute only.
A program may use at most 128 MiB of HBM per device.

v0:
```python
import functools
import jax
import jax.numpy as jnp
from jax import lax
from jax.experimental import pallas as pl
from jax.experimental.pallas import tpu as pltpu
from jax.sharding import PartitionSpec as P

BLOCKS = 2
SIDE = 4
PAD = 16
ENTRY = 16


def sweep_kernel(part, block, first, kt, local_rows, *refs):
    place, near_table, far_table, near, far, noise, scale = refs[:7]
    front = None if first else refs[7]
    out, front_out, out_buf, even, odd, out_sem = refs[-6:]
    steps, size = near.shape[1], near.shape[3]
    depth = kt * size
    width = even.shape[1]
    mine = pl.ds(block * width, width)

    def out_copy(s):
        return pltpu.make_async_copy(out_buf.at[s], out.at[s, mine], out_sem.at[s])

    def one_step(i, carry):
        s = steps - 1 - i
        row, picked, weight = [], [], []
        for table, tiles in ((near_table, near), (far_table, far)):
            for b in range(tiles.shape[0]):
                entry = (b * steps + s) * ENTRY
                for q in range(local_rows):
                    row.append(table[entry + local_rows * kt] * local_rows + q)
                    picked.append([even[table[entry + q * kt + k]] for k in range(kt)])
                    weight.append((tiles, b, q * depth))
        zero = jnp.zeros((width, size), jnp.bfloat16)

        def part_of(r, start, stop):
            tiles, b, base = weight[r]
            return tiles[b, s, base + start : base + stop]

        def product(left, right):
            return jnp.dot(left, right, preferred_element_type=jnp.float32)

        mixed = [None] * len(row)
        for r in range(0, len(row), 2):
            main = [
                product(jnp.concatenate(picked[r + j][:-1], axis=1), part_of(r + j, 0, depth - size))
                for j in range(2)
            ]
            last = product(
                jnp.concatenate(
                    [
                        jnp.concatenate([picked[r][-1], zero], axis=1),
                        jnp.concatenate([zero, picked[r + 1][-1]], axis=1),
                    ],
                    axis=0,
                ),
                jnp.concatenate([part_of(r, depth - size, depth), part_of(r + 1, depth - size, depth)], axis=0),
            )
            mixed[r] = main[0] + last[:width]
            mixed[r + 1] = main[1] + last[width:]
        for r, value in zip(row, mixed):
            lanes = pl.ds(pl.multiple_of(r * size, size), size)
            total = noise[s, mine, lanes].astype(jnp.float32) + value
            value = (scale[s, :, lanes] * total).astype(jnp.bfloat16)
            out_buf[s, :, lanes] = value
            odd[r] = value
        out_copy(s).start()
        even[...] = odd[...]
        return carry

    @pl.when(place[0] == part)
    def _active():
        even[...] = jnp.zeros(even.shape, even.dtype) if first else front[...]
        lax.fori_loop(0, steps, one_step, 0)
        front_out[...] = even[...]
        for s in range(steps):
            out_copy(s).wait()


def sweep(place, tables, tiles, noise, scale, front, out, part, block, kt, local_rows):
    steps, size = tiles[0].shape[1], tiles[0].shape[3]
    node_count = noise.shape[-1]
    width = noise.shape[1] // BLOCKS
    field = jax.ShapeDtypeStruct((node_count // size, width, size), jnp.bfloat16)
    anywhere = pl.BlockSpec(memory_space=pl.ANY)
    smem = pl.BlockSpec(memory_space=pltpu.SMEM)
    vmem = pl.BlockSpec(memory_space=pltpu.VMEM)
    more = [] if front is None else [front]
    specs = [smem, smem, smem, vmem, vmem, vmem, vmem] + [vmem] * len(more)
    aliases = {}
    if out is not None:
        aliases = {len(specs): 0}
        specs.append(anywhere)
        more.append(out)
    return pl.pallas_call(
        functools.partial(sweep_kernel, part, block, front is None, kt, local_rows),
        out_shape=(jax.ShapeDtypeStruct(noise.shape, noise.dtype), field),
        in_specs=specs,
        out_specs=(anywhere, vmem),
        input_output_aliases=aliases,
        scratch_shapes=[
            pltpu.VMEM((steps, width, node_count), jnp.bfloat16),
            pltpu.VMEM(field.shape, jnp.bfloat16),
            pltpu.VMEM(field.shape, jnp.bfloat16),
            pltpu.SemaphoreType.DMA((steps,)),
        ],
        compiler_params=pltpu.CompilerParams(vmem_limit_bytes=12 << 20),
        name="sweep",
    )(place, *tables, *tiles, noise, scale, *more)


def assemble_kernel(places, *refs):
    count = len(places)
    pieces, (target, table), pads, sems = refs[:count], refs[count : count + 2], refs[count + 2 : -1], refs[-1]
    steps, span, size = target.shape[1:]
    copies = []
    for i, (q, s) in enumerate(places):
        blocks, some = pieces[i].shape[:2]
        copies.append(pltpu.make_async_copy(pieces[i].at[:, :, pl.ds(span - PAD, PAD)], pads[i], sems.at[i, 0]))
        copies.append(
            pltpu.make_async_copy(pieces[i], target.at[pl.ds(q, blocks), pl.ds(s, some)], sems.at[i, 1])
        )
    for copy in copies:
        copy.start()
    for copy in copies[::2]:
        copy.wait()
    per_line = size // ENTRY
    where = {}
    for i, (q, s) in enumerate(places):
        for b in range(pads[i].shape[0]):
            for t in range(pads[i].shape[1]):
                where[(q + b) * steps + s + t] = pads[i], b, t
    for line in range(len(where) // per_line):
        value = jnp.zeros((1, size), jnp.float32)
        for j in range(per_line):
            buffer, b, t = where[line * per_line + j]
            entries = jnp.sum(buffer[b, t].astype(jnp.float32), axis=0, keepdims=True)
            value = value + (pltpu.roll(entries, j * ENTRY, 1) if j else entries)
        table[pl.ds(line, 1)] = value.astype(jnp.int32)
    for copy in copies[1::2]:
        copy.wait()


def assemble(pieces, places, blocks, steps):
    anywhere = pl.BlockSpec(memory_space=pl.ANY)
    span, size = pieces[0].shape[2:]
    bytes_moved = sum(p.size * 4 for p in pieces)
    tiles, table = pl.pallas_call(
        functools.partial(assemble_kernel, places),
        out_shape=(
            jax.ShapeDtypeStruct((blocks, steps, span, size), jnp.bfloat16),
            jax.ShapeDtypeStruct((blocks * steps * ENTRY // size, size), jnp.int32),
        ),
        in_specs=[anywhere] * len(pieces),
        out_specs=(anywhere, pl.BlockSpec(memory_space=pltpu.VMEM)),
        scratch_shapes=[pltpu.VMEM((*p.shape[:2], PAD, size), p.dtype) for p in pieces]
        + [pltpu.SemaphoreType.DMA((len(pieces), 2))],
        compiler_params=pltpu.CompilerParams(vmem_limit_bytes=2 << 20),
        cost_estimate=pl.CostEstimate(flops=0, bytes_accessed=bytes_moved, transcendentals=0),
        name="assemble",
    )(*pieces)
    return tiles, table.reshape(-1)


def moved(value, dx, dy):
    pairs = [
        (y * SIDE + x, (y + dy) % SIDE * SIDE + (x + dx) % SIDE) for y in range(SIDE) for x in range(SIDE)
    ]
    return lax.ppermute(value, "space", pairs)


def along(axis, by):
    return (by, 0) if axis == 0 else (0, by)


def ring_gather(block, first, second):
    low = moved(block, *along(first, 1))
    high = moved(block, *along(first, -1))
    far_low = moved(low[:, :1], *along(first, 1))
    far_high = moved(high[:, 1:], *along(first, -1))
    far = jnp.concatenate([far_low, far_high], axis=1)
    bundle = jnp.concatenate([block, low, high, far], axis=0)
    half = bundle.shape[0] // 2
    below = moved(bundle, *along(second, 1))
    above = moved(bundle, *along(second, -1))
    far_below = moved(below[:half], *along(second, 1))
    far_above = moved(above[half:], *along(second, -1))
    return (bundle, below, above), (far_below, far_above)


def on_device(noise, scale, tiles, columns):
    steps, local_samples, node_count = noise.shape
    local_rows, kt, size = tiles.shape[1:4]
    parts = lax.axis_size("tm")
    place = lax.axis_index("tm").astype(jnp.int32).reshape(1)
    spot = lax.axis_index("space").astype(jnp.int32)
    half = steps // 2
    scale_rows = scale.reshape(steps, 1, node_count)

    span = local_rows * kt * size + PAD
    turned = jnp.swapaxes(tiles, 3, 4).reshape(steps, span - PAD, size)
    entries = jnp.concatenate(
        [columns.reshape(steps, local_rows * kt), jnp.broadcast_to(spot, (steps, 1))], axis=1
    ).astype(jnp.bfloat16)
    entries = jnp.pad(entries[:, None], ((0, 0), (0, PAD - 1), (0, size - entries.shape[1])))
    block = jnp.concatenate([turned, entries], axis=1)[None]

    late_near, late_far = ring_gather(block[:, half:], 0, 1)
    early_near, early_far = ring_gather(block[:, :half], 1, 0)
    near, near_table = assemble(
        [pltpu.with_memory_space_constraint(p, pltpu.HBM) for p in (*late_near, *early_near)],
        [(i * SIDE, s) for s in (half, 0) for i in range(3)],
        3 * SIDE,
        steps,
    )
    far, far_table = assemble(
        (*late_far, *early_far), [(i * SIDE // 2, s) for s in (half, 0) for i in range(2)], SIDE, steps
    )
    tables, full = (near_table, far_table), (near, far)

    out = None
    fronts = [None] * BLOCKS
    for part in reversed(range(parts)):
        for block in range(BLOCKS):
            out, front = sweep(
                place, tables, full, noise, scale_rows, fronts[block], out, part, block, kt, local_rows
            )
            if part > 0:
                fronts[block] = lax.ppermute(front, "tm", [(part, part - 1)])
    return out


def solution(mesh):
    placed = (
        P("tm", "space", None),
        P("tm", None),
        P("tm", "space", None, None, None),
        P("tm", "space", None),
    )
    return jax.shard_map(
        on_device, mesh=mesh, in_specs=placed, out_specs=P("tm", "space", None), check_vma=False
    )
```

profile of v0, /device:TPU:0, one launch (start us, length us, event | category | flops | bytes accessed | tf_op | source)
XLA Modules:
  0.0 251.2 jit_solution(2900840227248276702)
XLA Ops:
  0.9 1.9 copy.23
  3.1 1.7 collective-permute-start.6
  4.8 1.6 collective-permute-start.7
  6.4 1.6 collective-permute-start
  8.0 1.7 collective-permute-start.1
  9.6 14.3 %collective-permute-done.6 = bf16[1,2,1552,128]{3,2,1,0:T(8,128)(2,1)S(1)} collective-permute-done((bf16[1,2,1552,128]{3,2,1,0:T(8,128)(2,1)S(1)}, bf16[1,2,1552,128]{3,2,1,0:T(8,128)(2,1)S(1)}, u32[]{:S(2)}, u32[]{:S(2)}) %collective-permute-start.6) | collective-permute-done | bytes 794656 | tf_op jit(solution)/shard_map/ppermute | solution.py:172
  24.4 3.0 %collective-permute-start.9 = (bf16[1,1,1552,128]{3,2,1,0:T(8,128)(2,1)S(1)}, bf16[1,1,1552,128]{3,2,1,0:T(8,128)(2,1)S(1)}, u32[]{:S(2)}, u32[]{:S(2)}) collective-permute-start(bf16[1,1,1552,128]{3,2,1,0:T(8,128)(2,1)S(1)} %slice.45), channel_id=1, source_target_pairs={{0,12},{1,13},{2,14},{3,15},{4,0},{5,1},{6,2},{7,3},{8,4},{9,5},{1... | collective-permute-start | bytes 1191944 | tf_op jit(solution)/shard_map/ppermute | solution.py:172
  27.4 1.6 collective-permute-start.2
  29.0 1.8 collective-permute-start.3
  30.8 4.7 %collective-permute-done.8 = bf16[1,1,1552,128]{3,2,1,0:T(8,128)(2,1)S(1)} collective-permute-done((bf16[1,1,1552,128]{3,2,1,0:T(8,128)(2,1)S(1)}, bf16[1,1,1552,128]{3,2,1,0:T(8,128)(2,1)S(1)}, u32[]{:S(2)}, u32[]{:S(2)}) %collective-permute-start.8) | collective-permute-done | bytes 397344 | tf_op jit(solution)/shard_map/ppermute | solution.py:172
  36.0 1.5 collective-permute-start.10
  37.5 1.8 collective-permute-start.11
  40.2 2.9 %collective-permute-start.5 = (bf16[4,2,1552,128]{3,2,1,0:T(8,128)(2,1)S(1)}, bf16[4,2,1552,128]{3,2,1,0:T(8,128)(2,1)S(1)}, u32[]{:S(2)}, u32[]{:S(2)}) collective-permute-start(bf16[4,2,1552,128]{3,2,1,0:T(8,128)(2,1)S(1)} %maximum_maximum_fusion.refs_0_), channel_id=1, source_target_pairs={{0,12},{1,13},{2,14},{3,15},{4,0},{5,1},{6,2},{7,3},{8,4},{9,5},{1... | collective-permute-start | bytes 9535496 | tf_op jit(solution)/shard_map/ppermute | solution.py:172
  43.1 63.4 %collective-permute-done.10.refs_4_ = bf16[4,2,1552,128]{3,2,1,0:T(8,128)(2,1)S(1)} collective-permute-done((bf16[4,2,1552,128]{3,2,1,0:T(8,128)(2,1)S(1)}, bf16[4,2,1552,128]{3,2,1,0:T(8,128)(2,1)S(1)}, u32[]{:S(2)}, u32[]{:S(2)}) %collective-permute-start.10) | collective-permute-done | bytes 3178528 | tf_op jit(solution)/shard_map/ppermute | solution.py:172
  106.5 1.4 slice.48
  108.0 1.3 slice.49
  109.4 3.0 %collective-permute-start.15 = (bf16[2,2,1552,128]{3,2,1,0:T(8,128)(2,1)}, bf16[2,2,1552,128]{3,2,1,0:T(8,128)(2,1)S(1)}, u32[]{:S(2)}, u32[]{:S(2)}) collective-permute-start(bf16[2,2,1552,128]{3,2,1,0:T(8,128)(2,1)} %slice.49), channel_id=1, source_target_pairs={{0,3},{1,0},{2,1},{3,2},{4,7},{5,4},{6,5},{7,6},{8,11},{9,8},{10,9... | collective-permute-start | bytes 4767752 | tf_op jit(solution)/shard_map/ppermute | solution.py:172
  112.4 1.4 slice.46
  113.8 0.8 copy-done.5
  114.7 1.4 slice.47
  116.9 2.5 collective-permute-start.13
  119.5 6.7 %assemble.2 = (bf16[12,4,1552,128]{3,2,1,0:T(8,128)(2,1)S(1)}, s32[6,128]{1,0:T(8,128)S(1)}) custom-call(bf16[4,2,1552,128]{3,2,1,0:T(8,128)(2,1)} %copy-done.2, bf16[4,2,1552,128]{3,2,1,0:T(8,128)(2,1)} %copy-done.5, bf16[4,2,1552,128]{3,2,1,0:T(8,128)(2,1)} %copy-done.6, bf16[4,2,1552,128]{3,2,1,0:T(8,128)(2,1)} %copy-done.1, ...), custom_call_target="tpu_custom_call" | custom-call | bytes 38141952 | tf_op jit(solution)/shard_map/assemble/pallas_call | solution.py:151
  126.2 17.3 %collective-permute-done.14.refs_2_ = bf16[2,2,1552,128]{3,2,1,0:T(8,128)(2,1)S(1)} collective-permute-done((bf16[2,2,1552,128]{3,2,1,0:T(8,128)(2,1)}, bf16[2,2,1552,128]{3,2,1,0:T(8,128)(2,1)S(1)}, u32[]{:S(2)}, u32[]{:S(2)}) %collective-permute-start.14) | collective-permute-done | bytes 1589280 | tf_op jit(solution)/shard_map/ppermute | solution.py:172
  144.2 4.8 %collective-permute-done.12.refs_0_ = bf16[2,2,1552,128]{3,2,1,0:T(8,128)(2,1)} collective-permute-done((bf16[2,2,1552,128]{3,2,1,0:T(8,128)(2,1)}, bf16[2,2,1552,128]{3,2,1,0:T(8,128)(2,1)}, u32[]{:S(2)}, u32[]{:S(2)}) %collective-permute-start.12) | collective-permute-done | bytes 1589280 | tf_op jit(solution)/shard_map/ppermute | solution.py:172
  149.0 1.9 collective-permute-done.13.refs_1_
  150.9 2.0 assemble.3
  166.7 0.9 sweep.26
  170.3 1.3 collective-permute-start.29
  172.3 1.3 collective-permute-start.28
  173.6 62.2 %collective-permute-done.29.refs_7_ = bf16[64,32,128]{2,1,0:T(8,128)(2,1)S(1)} collective-permute-done((bf16[64,32,128]{2,1,0:T(8,128)(2,1)S(1)}, bf16[64,32,128]{2,1,0:T(8,128)(2,1)S(1)}, u32[]{:S(2)}, u32[]{:S(2)}) %collective-permute-start.29) | collective-permute-done | bytes 524320 | tf_op jit(solution)/shard_map/ppermute | solution.py:232
  235.8 7.3 %sweep.30 = (bf16[4,64,8192]{2,1,0:T(8,128)(2,1)}, bf16[64,32,128]{2,1,0:T(8,128)(2,1)}) custom-call(s32[1]{0:T(128)} %bitcast.refs_0_, s32[768]{0:T(1024)S(1)} %bitcast.23, s32[256]{0:T(256)S(1)} %bitcast.39, bf16[12,4,1552,128]{3,2,1,0:T(8,128)(2,1)S(1)} %get-tuple-element.41.refs_3_, ...), custom_call_target="tpu_custom_call", output_to_operand_aliasing={{0}: (8, {})} | custom-call | tf_op jit(solution)/shard_map/sweep/pallas_call | solution.py:98
  243.7 7.3 %sweep.31 = (bf16[4,64,8192]{2,1,0:T(8,128)(2,1)}, bf16[64,32,128]{2,1,0:T(8,128)(2,1)}) custom-call(s32[1]{0:T(128)} %bitcast.refs_0_, s32[768]{0:T(1024)S(1)} %bitcast.24, s32[256]{0:T(256)S(1)} %bitcast.40, bf16[12,4,1552,128]{3,2,1,0:T(8,128)(2,1)S(1)} %get-tuple-element.41.refs_3_, ...), custom_call_target="tpu_custom_call", output_to_operand_aliasing={{0}: (8, {})} | custom-call | tf_op jit(solution)/shard_map/sweep/pallas_call | solution.py:98
  (81 shorter events, 22.3 us)
Async XLA Ops:
  3.1 20.9 %collective-permute-start.6 = (bf16[1,2,1552,128]{3,2,1,0:T(8,128)(2,1)S(1)}, bf16[1,2,1552,128]{3,2,1,0:T(8,128)(2,1)S(1)}, u32[]{:S(2)}, u32[]{:S(2)}) collective-permute-start(bf16[1,2,1552,128]{3,2,1,0:T(8,128)(2,1)S(1)} %get-tuple-element.73), channel_id=1, source_target_pairs={{0,4},{1,5},{2,6},{3,7},{4,8},{5,9},{6,10},{7,11},{8,12},{9,13},{1... | collective-permute-start | bytes 2383880 | tf_op jit(solution)/shard_map/ppermute | solution.py:172
  4.8 19.6 %collective-permute-start.7 = (bf16[1,2,1552,128]{3,2,1,0:T(8,128)(2,1)S(1)}, bf16[1,2,1552,128]{3,2,1,0:T(8,128)(2,1)S(1)}, u32[]{:S(2)}, u32[]{:S(2)}) collective-permute-start(bf16[1,2,1552,128]{3,2,1,0:T(8,128)(2,1)S(1)} %get-tuple-element.73), channel_id=1, source_target_pairs={{0,12},{1,13},{2,14},{3,15},{4,0},{5,1},{6,2},{7,3},{8,4},{9,5},{1... | collective-permute-start | bytes 2383880 | tf_op jit(solution)/shard_map/ppermute | solution.py:172
  6.4 21.0 %collective-permute-start = (bf16[1,2,1552,128]{3,2,1,0:T(8,128)(2,1)S(1)}, bf16[1,2,1552,128]{3,2,1,0:T(8,128)(2,1)S(1)}, u32[]{:S(2)}, u32[]{:S(2)}) collective-permute-start(bf16[1,2,1552,128]{3,2,1,0:T(8,128)(2,1)S(1)} %get-tuple-element.74), channel_id=1, source_target_pairs={{0,1},{1,2},{2,3},{3,0},{4,5},{5,6},{6,7},{7,4},{8,9},{9,10},{10,1... | collective-permute-start | bytes 2383880 | tf_op jit(solution)/shard_map/ppermute | solution.py:172
  8.0 21.0 %collective-permute-start.1 = (bf16[1,2,1552,128]{3,2,1,0:T(8,128)(2,1)S(1)}, bf16[1,2,1552,128]{3,2,1,0:T(8,128)(2,1)S(1)}, u32[]{:S(2)}, u32[]{:S(2)}) collective-permute-start(bf16[1,2,1552,128]{3,2,1,0:T(8,128)(2,1)S(1)} %get-tuple-element.74), channel_id=1, source_target_pairs={{0,3},{1,0},{2,1},{3,2},{4,7},{5,4},{6,5},{7,6},{8,11},{9,8},{10,9... | collective-permute-start | bytes 2383880 | tf_op jit(solution)/shard_map/ppermute | solution.py:172
  24.0 11.5 %collective-permute-start.8 = (bf16[1,1,1552,128]{3,2,1,0:T(8,128)(2,1)S(1)}, bf16[1,1,1552,128]{3,2,1,0:T(8,128)(2,1)S(1)}, u32[]{:S(2)}, u32[]{:S(2)}) collective-permute-start(bf16[1,1,1552,128]{3,2,1,0:T(8,128)(2,1)S(1)} %slice.44), channel_id=1, source_target_pairs={{0,4},{1,5},{2,6},{3,7},{4,8},{5,9},{6,10},{7,11},{8,12},{9,13},{1... | collective-permute-start | bytes 1191944 | tf_op jit(solution)/shard_map/ppermute | solution.py:172
  24.4 11.1 %collective-permute-start.9 = (bf16[1,1,1552,128]{3,2,1,0:T(8,128)(2,1)S(1)}, bf16[1,1,1552,128]{3,2,1,0:T(8,128)(2,1)S(1)}, u32[]{:S(2)}, u32[]{:S(2)}) collective-permute-start(bf16[1,1,1552,128]{3,2,1,0:T(8,128)(2,1)S(1)} %slice.45), channel_id=1, source_target_pairs={{0,12},{1,13},{2,14},{3,15},{4,0},{5,1},{6,2},{7,3},{8,4},{9,5},{1... | collective-permute-start | bytes 1191944 | tf_op jit(solution)/shard_map/ppermute | solution.py:172
  27.4 11.9 %collective-permute-start.2 = (bf16[1,1,1552,128]{3,2,1,0:T(8,128)(2,1)S(1)}, bf16[1,1,1552,128]{3,2,1,0:T(8,128)(2,1)S(1)}, u32[]{:S(2)}, u32[]{:S(2)}) collective-permute-start(bf16[1,1,1552,128]{3,2,1,0:T(8,128)(2,1)S(1)} %slice.41), channel_id=1, source_target_pairs={{0,1},{1,2},{2,3},{3,0},{4,5},{5,6},{6,7},{7,4},{8,9},{9,10},{10,1... | collective-permute-start | bytes 1191944 | tf_op jit(solution)/shard_map/ppermute | solution.py:172
  29.0 10.3 %collective-permute-start.3 = (bf16[1,1,1552,128]{3,2,1,0:T(8,128)(2,1)S(1)}, bf16[1,1,1552,128]{3,2,1,0:T(8,128)(2,1)S(1)}, u32[]{:S(2)}, u32[]{:S(2)}) collective-permute-start(bf16[1,1,1552,128]{3,2,1,0:T(8,128)(2,1)S(1)} %slice.42), channel_id=1, source_target_pairs={{0,3},{1,0},{2,1},{3,2},{4,7},{5,4},{6,5},{7,6},{8,11},{9,8},{10,9... | collective-permute-start | bytes 1191944 | tf_op jit(solution)/shard_map/ppermute | solution.py:172
  36.0 70.5 %collective-permute-start.10 = (bf16[4,2,1552,128]{3,2,1,0:T(8,128)(2,1)S(1)}, bf16[4,2,1552,128]{3,2,1,0:T(8,128)(2,1)S(1)}, u32[]{:S(2)}, u32[]{:S(2)}) collective-permute-start(bf16[4,2,1552,128]{3,2,1,0:T(8,128)(2,1)S(1)} %maximum_maximum_fusion.1.refs_3_), channel_id=1, source_target_pairs={{0,1},{1,2},{2,3},{3,0},{4,5},{5,6},{6,7},{7,4},{8,9},{9,10},{10,1... | collective-permute-start | bytes 9535496 | tf_op jit(solution)/shard_map/ppermute | solution.py:172
  37.5 70.6 %collective-permute-start.11 = (bf16[4,2,1552,128]{3,2,1,0:T(8,128)(2,1)S(1)}, bf16[4,2,1552,128]{3,2,1,0:T(8,128)(2,1)S(1)}, u32[]{:S(2)}, u32[]{:S(2)}) collective-permute-start(bf16[4,2,1552,128]{3,2,1,0:T(8,128)(2,1)S(1)} %maximum_maximum_fusion.1.refs_3_), channel_id=1, source_target_pairs={{0,3},{1,0},{2,1},{3,2},{4,7},{5,4},{6,5},{7,6},{8,11},{9,8},{10,9... | collective-permute-start | bytes 9535496 | tf_op jit(solution)/shard_map/ppermute | solution.py:172
  39.8 74.0 %copy-start.2 = (bf16[4,2,1552,128]{3,2,1,0:T(8,128)(2,1)}, bf16[4,2,1552,128]{3,2,1,0:T(8,128)(2,1)S(1)}, u32[]{:S(2)}) copy-start(bf16[4,2,1552,128]{3,2,1,0:T(8,128)(2,1)S(1)} %maximum_maximum_fusion.refs_0_) | copy-start | bytes 9535492
  39.8 72.6 %collective-permute-start.4 = (bf16[4,2,1552,128]{3,2,1,0:T(8,128)(2,1)S(1)}, bf16[4,2,1552,128]{3,2,1,0:T(8,128)(2,1)S(1)}, u32[]{:S(2)}, u32[]{:S(2)}) collective-permute-start(bf16[4,2,1552,128]{3,2,1,0:T(8,128)(2,1)S(1)} %maximum_maximum_fusion.refs_0_), channel_id=1, source_target_pairs={{0,4},{1,5},{2,6},{3,7},{4,8},{5,9},{6,10},{7,11},{8,12},{9,13},{1... | collective-permute-start | bytes 9535496 | tf_op jit(solution)/shard_map/ppermute | solution.py:172
  40.2 73.6 %collective-permute-start.5 = (bf16[4,2,1552,128]{3,2,1,0:T(8,128)(2,1)S(1)}, bf16[4,2,1552,128]{3,2,1,0:T(8,128)(2,1)S(1)}, u32[]{:S(2)}, u32[]{:S(2)}) collective-permute-start(bf16[4,2,1552,128]{3,2,1,0:T(8,128)(2,1)S(1)} %maximum_maximum_fusion.refs_0_), channel_id=1, source_target_pairs={{0,12},{1,13},{2,14},{3,15},{4,0},{5,1},{6,2},{7,3},{8,4},{9,5},{1... | collective-permute-start | bytes 9535496 | tf_op jit(solution)/shard_map/ppermute | solution.py:172
  107.9 35.7 %collective-permute-start.14 = (bf16[2,2,1552,128]{3,2,1,0:T(8,128)(2,1)}, bf16[2,2,1552,128]{3,2,1,0:T(8,128)(2,1)S(1)}, u32[]{:S(2)}, u32[]{:S(2)}) collective-permute-start(bf16[2,2,1552,128]{3,2,1,0:T(8,128)(2,1)} %slice.48), channel_id=1, source_target_pairs={{0,1},{1,2},{2,3},{3,0},{4,5},{5,6},{6,7},{7,4},{8,9},{9,10},{10,1... | collective-permute-start | bytes 4767752 | tf_op jit(solution)/shard_map/ppermute | solution.py:172
  109.4 34.8 %collective-permute-start.15 = (bf16[2,2,1552,128]{3,2,1,0:T(8,128)(2,1)}, bf16[2,2,1552,128]{3,2,1,0:T(8,128)(2,1)S(1)}, u32[]{:S(2)}, u32[]{:S(2)}) collective-permute-start(bf16[2,2,1552,128]{3,2,1,0:T(8,128)(2,1)} %slice.49), channel_id=1, source_target_pairs={{0,3},{1,0},{2,1},{3,2},{4,7},{5,4},{6,5},{7,6},{8,11},{9,8},{10,9... | collective-permute-start | bytes 4767752 | tf_op jit(solution)/shard_map/ppermute | solution.py:172
  113.8 35.2 %collective-permute-start.12 = (bf16[2,2,1552,128]{3,2,1,0:T(8,128)(2,1)}, bf16[2,2,1552,128]{3,2,1,0:T(8,128)(2,1)}, u32[]{:S(2)}, u32[]{:S(2)}) collective-permute-start(bf16[2,2,1552,128]{3,2,1,0:T(8,128)(2,1)} %slice.46), channel_id=1, source_target_pairs={{0,4},{1,5},{2,6},{3,7},{4,8},{5,9},{6,10},{7,11},{8,12},{9,13},{1... | collective-permute-start | bytes 4767752 | tf_op jit(solution)/shard_map/ppermute | solution.py:172
  116.9 34.0 %collective-permute-start.13 = (bf16[2,2,1552,128]{3,2,1,0:T(8,128)(2,1)}, bf16[2,2,1552,128]{3,2,1,0:T(8,128)(2,1)}, u32[]{:S(2)}, u32[]{:S(2)}) collective-permute-start(bf16[2,2,1552,128]{3,2,1,0:T(8,128)(2,1)} %slice.47), channel_id=1, source_target_pairs={{0,12},{1,13},{2,14},{3,15},{4,0},{5,1},{6,2},{7,3},{8,4},{9,5},{1... | collective-permute-start | bytes 4767752 | tf_op jit(solution)/shard_map/ppermute | solution.py:172
  126.2 26.8 %copy-start = (bf16[4,64,8192]{2,1,0:T(8,128)(2,1)S(1)}, bf16[4,64,8192]{2,1,0:T(8,128)(2,1)}, u32[]{:S(2)}) copy-start(bf16[4,64,8192]{2,1,0:T(8,128)(2,1)} %refs_5_.31) | copy-start | bytes 12582916
  153.6 2.1 collective-permute-start.17
  154.9 2.2 collective-permute-start.16
  156.5 2.1 collective-permute-start.19
  157.8 2.1 collective-permute-start.18
  159.2 2.1 collective-permute-start.21
  160.6 2.1 collective-permute-start.20
  161.9 2.1 collective-permute-start.23
  163.3 2.1 collective-permute-start.22
  164.7 2.1 collective-permute-start.25
  166.0 2.3 collective-permute-start.24
  167.6 2.1 collective-permute-start.27
  169.0 2.7 %collective-permute-start.26 = (bf16[64,32,128]{2,1,0:T(8,128)(2,1)S(1)}, bf16[64,32,128]{2,1,0:T(8,128)(2,1)S(1)}, u32[]{:S(2)}, u32[]{:S(2)}) collective-permute-start(bf16[64,32,128]{2,1,0:T(8,128)(2,1)S(1)} %get-tuple-element.64), channel_id=1, source_target_pairs={{32,16},{33,17},{34,18},{35,19},{36,20},{37,21},{38,22},{39,23},{4... | collective-permute-start | bytes 1572872 | tf_op jit(solution)/shard_map/ppermute | solution.py:232
  170.3 65.5 %collective-permute-start.29 = (bf16[64,32,128]{2,1,0:T(8,128)(2,1)S(1)}, bf16[64,32,128]{2,1,0:T(8,128)(2,1)S(1)}, u32[]{:S(2)}, u32[]{:S(2)}) collective-permute-start(bf16[64,32,128]{2,1,0:T(8,128)(2,1)S(1)} %get-tuple-element.69), channel_id=1, source_target_pairs={{16,0},{17,1},{18,2},{19,3},{20,4},{21,5},{22,6},{23,7},{24,8},{25... | collective-permute-start | bytes 1572872 | tf_op jit(solution)/shard_map/ppermute | solution.py:232
  172.3 71.4 %collective-permute-start.28 = (bf16[64,32,128]{2,1,0:T(8,128)(2,1)S(1)}, bf16[64,32,128]{2,1,0:T(8,128)(2,1)S(1)}, u32[]{:S(2)}, u32[]{:S(2)}) collective-permute-start(bf16[64,32,128]{2,1,0:T(8,128)(2,1)S(1)} %get-tuple-element.68), channel_id=1, source_target_pairs={{16,0},{17,1},{18,2},{19,3},{20,4},{21,5},{22,6},{23,7},{24,8},{25... | collective-permute-start | bytes 1572872 | tf_op jit(solution)/shard_map/ppermute | solution.py:232
  (6 other events, 33.6 us)
where the time goes:
time: 251 us
  waiting for transfers between devices  170 us (68%)
  starting transfers between devices  36.5 us (15%)
  Pallas kernels  32.7 us (13%)
  local copies, waits for them, and re-layouts  9.62 us (4%)
    ppermute x16, waiting for transfers between devices, moved(): return lax.ppermute(value, 'space', pairs)  107 us
    ppermute x14, waiting for transfers between devices, on_device(): fronts[block] = lax.ppermute(front, 'tm', [(part, part - 1)])  62.8 us
    ppermute x16, starting transfers between devices, moved(): return lax.ppermute(value, 'space', pairs)  25.6 us
    pallas_call x16, Pallas kernels, sweep(): pl.pallas_call(functools.partial(sweep_kernel, part, block, front is None...  24 us
    ppermute x14, starting transfers between devices, on_device(): fronts[block] = lax.ppermute(front, 'tm', [(part, part - 1)])  10.9 us
    pallas_call x2, Pallas kernels, assemble(): pl.pallas_call(functools.partial(assemble_kernel, places), out_shape=(jax...  8.68 us
  transfers between devices with their start and end apart: 30, of which 9 were waited for; matrix products, arithmetic and copies ran while one was open for 3% of the time, Pallas kernels for 9%

commit v1 on v0

--- a/solution.py
+++ b/solution.py
@@ -12,24 +12,41 @@
 ENTRY = 16
 
 
-def sweep_kernel(part, block, first, kt, local_rows, *refs):
-    place, near_table, far_table, near, far, noise, scale = refs[:7]
-    front = None if first else refs[7]
-    out, front_out, out_buf, even, odd, out_sem = refs[-6:]
+def sweep_kernel(part, block, before, first, ends, kt, local_rows, *refs):
+    table, near, far, noise, scale = refs[:5]
+    refs = list(refs[5:])
+    front = None if first else refs.pop(0)
+    tail = None if before is None else refs.pop(0)
+    if before is not None:
+        refs.pop(0)
+    out = refs.pop(0)
+    front_out, tail_out = (None, None) if ends else (refs.pop(0), None)
+    if not (part == 0 and block == BLOCKS - 1):
+        tail_out = refs.pop(0)
+    out_buf, even, odd, out_sem, tail_sem = refs
     steps, size = near.shape[1], near.shape[3]
     depth = kt * size
     width = even.shape[1]
     mine = pl.ds(block * width, width)
+    here = table[local_rows * kt + 1]
 
     def out_copy(s):
         return pltpu.make_async_copy(out_buf.at[s], out.at[s, mine], out_sem.at[s])
+
+    def flush(action):
+        if before is not None:
+            held = pl.ds(before[1] * width, width)
+
+            @pl.when(here == before[0])
+            def _flush():
+                action(pltpu.make_async_copy(tail, out.at[0, held], tail_sem.at[0]))
 
     def one_step(i, carry):
         s = steps - 1 - i
         row, picked, weight = [], [], []
-        for table, tiles in ((near_table, near), (far_table, far)):
+        for base, tiles in ((0, near), (near.shape[0], far)):
             for b in range(tiles.shape[0]):
-                entry = (b * steps + s) * ENTRY
+                entry = ((base + b) * steps + s) * ENTRY
                 for q in range(local_rows):
                     row.append(table[entry + local_rows * kt] * local_rows + q)
                     picked.append([even[table[entry + q * kt + k]] for k in range(kt)])
@@ -67,20 +84,34 @@
             value = (scale[s, :, lanes] * total).astype(jnp.bfloat16)
             out_buf[s, :, lanes] = value
             odd[r] = value
-        out_copy(s).start()
-        even[...] = odd[...]
+
+        @pl.when(i < steps - 1)
+        def _next():
+            out_copy(s).start()
+            even[...] = odd[...]
+
         return carry
 
-    @pl.when(place[0] == part)
+    flush(lambda copy: copy.start())
+
+    @pl.when(here == part)
     def _active():
         even[...] = jnp.zeros(even.shape, even.dtype) if first else front[...]
         lax.fori_loop(0, steps, one_step, 0)
-        front_out[...] = even[...]
-        for s in range(steps):
+        if front_out is not None:
+            front_out[...] = odd[...]
+        if tail_out is None:
+            out_copy(0).start()
+            out_copy(0).wait()
+        else:
+            tail_out[...] = out_buf[0]
+        for s in range(1, steps):
             out_copy(s).wait()
 
-
-def sweep(place, tables, tiles, noise, scale, front, out, part, block, kt, local_rows):
+    flush(lambda copy: copy.wait())
+
+
+def sweep(table, tiles, noise, scale, front, tail, out, part, block, before, kt, local_rows):
     steps, size = tiles[0].shape[1], tiles[0].shape[3]
     node_count = noise.shape[-1]
     width = noise.shape[1] // BLOCKS
@@ -88,33 +119,46 @@
     anywhere = pl.BlockSpec(memory_space=pl.ANY)
     smem = pl.BlockSpec(memory_space=pltpu.SMEM)
     vmem = pl.BlockSpec(memory_space=pltpu.VMEM)
-    more = [] if front is None else [front]
-    specs = [smem, smem, smem, vmem, vmem, vmem, vmem] + [vmem] * len(more)
+    more = [value for value in (front, tail) if value is not None]
+    specs = [smem, vmem, vmem, vmem, vmem] + [vmem] * len(more)
     aliases = {}
     if out is not None:
         aliases = {len(specs): 0}
         specs.append(anywhere)
         more.append(out)
-    return pl.pallas_call(
-        functools.partial(sweep_kernel, part, block, front is None, kt, local_rows),
-        out_shape=(jax.ShapeDtypeStruct(noise.shape, noise.dtype), field),
+    shapes, places = [jax.ShapeDtypeStruct(noise.shape, noise.dtype)], [anywhere]
+    if part > 0:
+        shapes.append(field)
+        places.append(vmem)
+    if part > 0 or block < BLOCKS - 1:
+        shapes.append(jax.ShapeDtypeStruct((width, node_count), jnp.bfloat16))
+        places.append(vmem)
+    results = pl.pallas_call(
+        functools.partial(sweep_kernel, part, block, before, front is None, part == 0, kt, local_rows),
+        out_shape=tuple(shapes),
         in_specs=specs,
-        out_specs=(anywhere, vmem),
+        out_specs=tuple(places),
         input_output_aliases=aliases,
         scratch_shapes=[
             pltpu.VMEM((steps, width, node_count), jnp.bfloat16),
             pltpu.VMEM(field.shape, jnp.bfloat16),
             pltpu.VMEM(field.shape, jnp.bfloat16),
             pltpu.SemaphoreType.DMA((steps,)),
+            pltpu.SemaphoreType.DMA((1,)),
         ],
         compiler_params=pltpu.CompilerParams(vmem_limit_bytes=12 << 20),
         name="sweep",
-    )(place, *tables, *tiles, noise, scale, *more)
+    )(table, *tiles, noise, scale, *more)
+    results = list(results)
+    out = results.pop(0)
+    front = results.pop(0) if part > 0 else None
+    return out, front, results.pop(0) if results else None
 
 
 def assemble_kernel(places, *refs):
     count = len(places)
-    pieces, (target, table), pads, sems = refs[:count], refs[count : count + 2], refs[count + 2 : -1], refs[-1]
+    sems, pads = refs[-1], refs[-1 - count : -1]
+    pieces, earlier, (target, table) = refs[:count], refs[count : -3 - count], refs[-3 - count : -1 - count]
     steps, span, size = target.shape[1:]
     copies = []
     for i, (q, s) in enumerate(places):
@@ -128,6 +172,9 @@
     for copy in copies[::2]:
         copy.wait()
     per_line = size // ENTRY
+    skip = earlier[0].shape[0] if earlier else 0
+    if earlier:
+        table[pl.ds(0, skip)] = earlier[0][...]
     where = {}
     for i, (q, s) in enumerate(places):
         for b in range(pads[i].shape[0]):
@@ -139,30 +186,31 @@
             buffer, b, t = where[line * per_line + j]
             entries = jnp.sum(buffer[b, t].astype(jnp.float32), axis=0, keepdims=True)
             value = value + (pltpu.roll(entries, j * ENTRY, 1) if j else entries)
-        table[pl.ds(line, 1)] = value.astype(jnp.int32)
+        table[pl.ds(skip + line, 1)] = value.astype(jnp.int32)
     for copy in copies[1::2]:
         copy.wait()
 
 
-def assemble(pieces, places, blocks, steps):
+def assemble(pieces, places, blocks, steps, earlier=()):
     anywhere = pl.BlockSpec(memory_space=pl.ANY)
     span, size = pieces[0].shape[2:]
     bytes_moved = sum(p.size * 4 for p in pieces)
-    tiles, table = pl.pallas_call(
+    lines = blocks * steps * ENTRY // size + sum(e.shape[0] for e in earlier)
+    vmem = pl.BlockSpec(memory_space=pltpu.VMEM)
+    return pl.pallas_call(
         functools.partial(assemble_kernel, places),
         out_shape=(
             jax.ShapeDtypeStruct((blocks, steps, span, size), jnp.bfloat16),
-            jax.ShapeDtypeStruct((blocks * steps * ENTRY // size, size), jnp.int32),
+            jax.ShapeDtypeStruct((lines, size), jnp.int32),
         ),
-        in_specs=[anywhere] * len(pieces),
-        out_specs=(anywhere, pl.BlockSpec(memory_space=pltpu.VMEM)),
+        in_specs=[anywhere] * len(pieces) + [vmem] * len(earlier),
+        out_specs=(anywhere, vmem),
         scratch_shapes=[pltpu.VMEM((*p.shape[:2], PAD, size), p.dtype) for p in pieces]
         + [pltpu.SemaphoreType.DMA((len(pieces), 2))],
         compiler_params=pltpu.CompilerParams(vmem_limit_bytes=2 << 20),
         cost_estimate=pl.CostEstimate(flops=0, bytes_accessed=bytes_moved, transcendentals=0),
         name="assemble",
-    )(*pieces)
-    return tiles, table.reshape(-1)
+    )(*pieces, *earlier)
 
 
 def moved(value, dx, dy):
@@ -195,15 +243,14 @@
     steps, local_samples, node_count = noise.shape
     local_rows, kt, size = tiles.shape[1:4]
     parts = lax.axis_size("tm")
-    place = lax.axis_index("tm").astype(jnp.int32).reshape(1)
-    spot = lax.axis_index("space").astype(jnp.int32)
+    spot = jnp.stack([lax.axis_index("space"), lax.axis_index("tm")]).astype(jnp.int32)
     half = steps // 2
     scale_rows = scale.reshape(steps, 1, node_count)
 
     span = local_rows * kt * size + PAD
     turned = jnp.swapaxes(tiles, 3, 4).reshape(steps, span - PAD, size)
     entries = jnp.concatenate(
-        [columns.reshape(steps, local_rows * kt), jnp.broadcast_to(spot, (steps, 1))], axis=1
+        [columns.reshape(steps, local_rows * kt), jnp.broadcast_to(spot, (steps, 2))], axis=1
     ).astype(jnp.bfloat16)
     entries = jnp.pad(entries[:, None], ((0, 0), (0, PAD - 1), (0, size - entries.shape[1])))
     block = jnp.concatenate([turned, entries], axis=1)[None]
@@ -216,18 +263,23 @@
         3 * SIDE,
         steps,
     )
-    far, far_table = assemble(
-        (*late_far, *early_far), [(i * SIDE // 2, s) for s in (half, 0) for i in range(2)], SIDE, steps
-    )
-    tables, full = (near_table, far_table), (near, far)
-
-    out = None
+    far, table = assemble(
+        (*late_far, *early_far),
+        [(i * SIDE // 2, s) for s in (half, 0) for i in range(2)],
+        SIDE,
+        steps,
+        (near_table,),
+    )
+    table, full = table.reshape(-1), (near, far)
+
+    out = tail = before = None
     fronts = [None] * BLOCKS
     for part in reversed(range(parts)):
         for block in range(BLOCKS):
-            out, front = sweep(
-                place, tables, full, noise, scale_rows, fronts[block], out, part, block, kt, local_rows
+            out, front, tail = sweep(
+                table, full, noise, scale_rows, fronts[block], tail, out, part, block, before, kt, local_rows
             )
+            before = (part, block)
             if part > 0:
                 fronts[block] = lax.ppermute(front, "tm", [(part, part - 1)])
     return out

time: 251 us -> 240 us (0.956)
  waiting for transfers between devices: 170 us -> 165 us
  local copies, waits for them, and re-layouts: 9.62 us -> 5.72 us
  Pallas kernels: 32.7 us -> 29.1 us
    ppermute x14, waiting for transfers between devices: 62.8 us -> 57.8 us  [on_device(): fronts[block] = lax.ppermute(front, 'tm', [(part, part - 1)])]
    slice x2, local copies, waits for them, and re-layouts: 2.76 us -> 0.21 us  [ring_gather(): far_above = moved(above[half:], *along(second, -1))]
  transfers between devices with their start and end apart: 30 -> 30, of which waited for: 9 -> 7; matrix products, arithmetic and copies ran while one was open for 3% -> 1% of each run, Pallas kernels for 9% -> 9%
where the time goes in v1:
time: 240 us
  waiting for transfers between devices  165 us (69%)
  starting transfers between devices  37.5 us (16%)
  Pallas kernels  29.1 us (12%)
  local copies, waits for them, and re-layouts  5.72 us (2%)
    ppermute x16, waiting for transfers between devices, moved(): return lax.ppermute(value, 'space', pairs)  107 us
    ppermute x14, waiting for transfers between devices, on_device(): fronts[block] = lax.ppermute(front, 'tm', [(part, part - 1)])  57.8 us
    ppermute x16, starting transfers between devices, moved(): return lax.ppermute(value, 'space', pairs)  26.6 us
    pallas_call x16, Pallas kernels, sweep(): pl.pallas_call(functools.partial(sweep_kernel, part, block, before, front...  21.7 us
    ppermute x14, starting transfers between devices, on_device(): fronts[block] = lax.ppermute(front, 'tm', [(part, part - 1)])  10.9 us
    pallas_call x2, Pallas kernels, assemble(): pl.pallas_call(functools.partial(assemble_kernel, places), out_shape=(jax...  7.34 us
  transfers between devices with their start and end apart: 30, of which 7 were waited for; matrix products, arithmetic and copies ran while one was open for 1% of the time, Pallas kernels for 9%

profile of v1, /device:TPU:0, one launch (start us, length us, event | category | flops | bytes accessed | tf_op | source)
XLA Modules:
  0.0 239.7 jit_solution(471505154720091329)
XLA Ops:
  0.0 0.7 convert.8
  0.9 1.9 copy.23
  3.2 1.7 collective-permute-start.8
  5.0 1.6 collective-permute-start.9
  6.5 1.6 collective-permute-start
  8.1 1.7 collective-permute-start.1
  9.8 14.3 %collective-permute-done.8 = bf16[1,2,1552,128]{3,2,1,0:T(8,128)(2,1)S(1)} collective-permute-done((bf16[1,2,1552,128]{3,2,1,0:T(8,128)(2,1)S(1)}, bf16[1,2,1552,128]{3,2,1,0:T(8,128)(2,1)S(1)}, u32[]{:S(2)}, u32[]{:S(2)}) %collective-permute-start.8) | collective-permute-done | bytes 794656 | tf_op jit(solution)/shard_map/ppermute | solution.py:220
  24.5 3.0 %collective-permute-start.11 = (bf16[1,1,1552,128]{3,2,1,0:T(8,128)(2,1)S(1)}, bf16[1,1,1552,128]{3,2,1,0:T(8,128)(2,1)S(1)}, u32[]{:S(2)}, u32[]{:S(2)}) collective-permute-start(bf16[1,1,1552,128]{3,2,1,0:T(8,128)(2,1)S(1)} %slice.47), channel_id=1, source_target_pairs={{0,12},{1,13},{2,14},{3,15},{4,0},{5,1},{6,2},{7,3},{8,4},{9,5},{1... | collective-permute-start | bytes 1191944 | tf_op jit(solution)/shard_map/ppermute | solution.py:220
  27.6 1.6 collective-permute-start.2
  29.2 1.8 collective-permute-start.3
  31.0 4.7 %collective-permute-done.10 = bf16[1,1,1552,128]{3,2,1,0:T(8,128)(2,1)S(1)} collective-permute-done((bf16[1,1,1552,128]{3,2,1,0:T(8,128)(2,1)S(1)}, bf16[1,1,1552,128]{3,2,1,0:T(8,128)(2,1)S(1)}, u32[]{:S(2)}, u32[]{:S(2)}) %collective-permute-start.10) | collective-permute-done | bytes 397344 | tf_op jit(solution)/shard_map/ppermute | solution.py:220
  36.1 1.5 collective-permute-start.12
  37.6 1.8 collective-permute-start.14
  40.4 2.9 %collective-permute-start.6 = (bf16[4,2,1552,128]{3,2,1,0:T(8,128)(2,1)S(1)}, bf16[4,2,1552,128]{3,2,1,0:T(8,128)(2,1)S(1)}, u32[]{:S(2)}, u32[]{:S(2)}) collective-permute-start(bf16[4,2,1552,128]{3,2,1,0:T(8,128)(2,1)S(1)} %maximum_maximum_fusion.refs_0_), channel_id=1, source_target_pairs={{0,12},{1,13},{2,14},{3,15},{4,0},{5,1},{6,2},{7,3},{8,4},{9,5},{1... | collective-permute-start | bytes 9535496 | tf_op jit(solution)/shard_map/ppermute | solution.py:220
  43.3 63.4 %collective-permute-done.12.refs_4_ = bf16[4,2,1552,128]{3,2,1,0:T(8,128)(2,1)S(1)} collective-permute-done((bf16[4,2,1552,128]{3,2,1,0:T(8,128)(2,1)S(1)}, bf16[4,2,1552,128]{3,2,1,0:T(8,128)(2,1)S(1)}, u32[]{:S(2)}, u32[]{:S(2)}) %collective-permute-start.12) | collective-permute-done | bytes 3178528 | tf_op jit(solution)/shard_map/ppermute | solution.py:220
  106.7 1.4 slice.48
  108.3 3.1 %collective-permute-start.15 = (bf16[2,2,1552,128]{3,2,1,0:T(8,128)(2,1)S(1)}, bf16[2,2,1552,128]{3,2,1,0:T(8,128)(2,1)S(1)}, u32[]{:S(2)}, u32[]{:S(2)}) collective-permute-start(bf16[2,2,1552,128]{3,2,1,0:T(8,128)(2,1)S(1)} %slice.49), channel_id=1, source_target_pairs={{0,3},{1,0},{2,1},{3,2},{4,7},{5,4},{6,5},{7,6},{8,11},{9,8},{10,9... | collective-permute-start | bytes 4767752 | tf_op jit(solution)/shard_map/ppermute | solution.py:220
  111.8 3.3 %collective-permute-start.7 = (bf16[2,2,1552,128]{3,2,1,0:T(8,128)(2,1)S(1)}, bf16[2,2,1552,128]{3,2,1,0:T(8,128)(2,1)S(1)}, u32[]{:S(2)}, u32[]{:S(2)}) collective-permute-start(bf16[2,2,1552,128]{3,2,1,0:T(8,128)(2,1)S(1)} %slice.44), channel_id=1, source_target_pairs={{0,12},{1,13},{2,14},{3,15},{4,0},{5,1},{6,2},{7,3},{8,4},{9,5},{1... | collective-permute-start | bytes 4767752 | tf_op jit(solution)/shard_map/ppermute | solution.py:220
  115.2 6.7 %assemble.2 = (bf16[12,4,1552,128]{3,2,1,0:T(8,128)(2,1)S(1)}, s32[6,128]{1,0:T(8,128)S(1)}) custom-call(bf16[4,2,1552,128]{3,2,1,0:T(8,128)(2,1)} %copy-done.2, bf16[4,2,1552,128]{3,2,1,0:T(8,128)(2,1)} %copy-done.5, bf16[4,2,1552,128]{3,2,1,0:T(8,128)(2,1)} %copy-done.6, bf16[4,2,1552,128]{3,2,1,0:T(8,128)(2,1)} %copy-done.1, ...), custom_call_target="tpu_custom_call" | custom-call | bytes 38141952 | tf_op jit(solution)/shard_map/assemble/pallas_call | solution.py:200
  121.9 21.8 %collective-permute-done.13.refs_2_ = bf16[2,2,1552,128]{3,2,1,0:T(8,128)(2,1)S(1)} collective-permute-done((bf16[2,2,1552,128]{3,2,1,0:T(8,128)(2,1)}, bf16[2,2,1552,128]{3,2,1,0:T(8,128)(2,1)S(1)}, u32[]{:S(2)}, u32[]{:S(2)}) %collective-permute-start.13) | collective-permute-done | bytes 1589280 | tf_op jit(solution)/shard_map/ppermute | solution.py:220
  143.7 2.9 %collective-permute-done.5.refs_0_ = bf16[2,2,1552,128]{3,2,1,0:T(8,128)(2,1)S(1)} collective-permute-done((bf16[2,2,1552,128]{3,2,1,0:T(8,128)(2,1)S(1)}, bf16[2,2,1552,128]{3,2,1,0:T(8,128)(2,1)S(1)}, u32[]{:S(2)}, u32[]{:S(2)}) %collective-permute-start.5) | collective-permute-done | bytes 1589280 | tf_op jit(solution)/shard_map/ppermute | solution.py:220
  147.2 1.5 copy-done
  150.8 0.7 collective-permute-start.16
  151.5 0.8 sweep.18
  155.1 0.7 collective-permute-start.21
  162.7 0.9 sweep.26
  166.4 1.3 collective-permute-start.29
  168.3 1.3 collective-permute-start.28
  169.6 56.4 %collective-permute-done.29.refs_5_ = bf16[64,32,128]{2,1,0:T(8,128)(2,1)S(1)} collective-permute-done((bf16[64,32,128]{2,1,0:T(8,128)(2,1)S(1)}, bf16[64,32,128]{2,1,0:T(8,128)(2,1)S(1)}, u32[]{:S(2)}, u32[]{:S(2)}) %collective-permute-start.29) | collective-permute-done | bytes 524320 | tf_op jit(solution)/shard_map/ppermute | solution.py:284
  226.0 5.7 %sweep.30 = (bf16[4,64,8192]{2,1,0:T(8,128)(2,1)}, bf16[32,8192]{1,0:T(8,128)(2,1)S(1)}) custom-call(s32[1024]{0:T(1024)S(1)} %bitcast.21, bf16[12,4,1552,128]{3,2,1,0:T(8,128)(2,1)S(1)} %get-tuple-element.55.refs_1_, bf16[4,4,1552,128]{3,2,1,0:T(8,128)(2,1)S(1)} %get-tuple-element.56.refs_2_, ...), custom_call_target="tpu_custom_call", output_to_operand_aliasing={{0}: (7, {})} | custom-call | tf_op jit(solution)/shard_map/sweep/pallas_call | solution.py:136
  231.7 1.4 collective-permute-done.28.refs_5_
  233.1 6.4 %sweep.31 = bf16[4,64,8192]{2,1,0:T(8,128)(2,1)} custom-call(s32[1024]{0:T(1024)S(1)} %bitcast.22, bf16[12,4,1552,128]{3,2,1,0:T(8,128)(2,1)S(1)} %get-tuple-element.55.refs_1_, bf16[4,4,1552,128]{3,2,1,0:T(8,128)(2,1)S(1)} %get-tuple-element.56.refs_2_, bf16[4,64,8192]{2,1,0:T(8,128)(2,1)S(1)} %copy-done, ...), custom_call_target="tpu_custom_call", output_to_operand_aliasing={{}: (7, {})} | custom-call | tf_op jit(solution)/shard_map/sweep/pallas_call | solution.py:136
  (82 shorter events, 18.7 us)
Async XLA Ops:
  3.2 20.9 %collective-permute-start.8 = (bf16[1,2,1552,128]{3,2,1,0:T(8,128)(2,1)S(1)}, bf16[1,2,1552,128]{3,2,1,0:T(8,128)(2,1)S(1)}, u32[]{:S(2)}, u32[]{:S(2)}) collective-permute-start(bf16[1,2,1552,128]{3,2,1,0:T(8,128)(2,1)S(1)} %get-tuple-element.101), channel_id=1, source_target_pairs={{0,4},{1,5},{2,6},{3,7},{4,8},{5,9},{6,10},{7,11},{8,12},{9,13},{1... | collective-permute-start | bytes 2383880 | tf_op jit(solution)/shard_map/ppermute | solution.py:220
  5.0 19.6 %collective-permute-start.9 = (bf16[1,2,1552,128]{3,2,1,0:T(8,128)(2,1)S(1)}, bf16[1,2,1552,128]{3,2,1,0:T(8,128)(2,1)S(1)}, u32[]{:S(2)}, u32[]{:S(2)}) collective-permute-start(bf16[1,2,1552,128]{3,2,1,0:T(8,128)(2,1)S(1)} %get-tuple-element.101), channel_id=1, source_target_pairs={{0,12},{1,13},{2,14},{3,15},{4,0},{5,1},{6,2},{7,3},{8,4},{9,5},{1... | collective-permute-start | bytes 2383880 | tf_op jit(solution)/shard_map/ppermute | solution.py:220
  6.5 21.0 %collective-permute-start = (bf16[1,2,1552,128]{3,2,1,0:T(8,128)(2,1)S(1)}, bf16[1,2,1552,128]{3,2,1,0:T(8,128)(2,1)S(1)}, u32[]{:S(2)}, u32[]{:S(2)}) collective-permute-start(bf16[1,2,1552,128]{3,2,1,0:T(8,128)(2,1)S(1)} %get-tuple-element.102), channel_id=1, source_target_pairs={{0,1},{1,2},{2,3},{3,0},{4,5},{5,6},{6,7},{7,4},{8,9},{9,10},{10,1... | collective-permute-start | bytes 2383880 | tf_op jit(solution)/shard_map/ppermute | solution.py:220
  8.1 21.0 %collective-permute-start.1 = (bf16[1,2,1552,128]{3,2,1,0:T(8,128)(2,1)S(1)}, bf16[1,2,1552,128]{3,2,1,0:T(8,128)(2,1)S(1)}, u32[]{:S(2)}, u32[]{:S(2)}) collective-permute-start(bf16[1,2,1552,128]{3,2,1,0:T(8,128)(2,1)S(1)} %get-tuple-element.102), channel_id=1, source_target_pairs={{0,3},{1,0},{2,1},{3,2},{4,7},{5,4},{6,5},{7,6},{8,11},{9,8},{10,9... | collective-permute-start | bytes 2383880 | tf_op jit(solution)/shard_map/ppermute | solution.py:220
  24.1 11.5 %collective-permute-start.10 = (bf16[1,1,1552,128]{3,2,1,0:T(8,128)(2,1)S(1)}, bf16[1,1,1552,128]{3,2,1,0:T(8,128)(2,1)S(1)}, u32[]{:S(2)}, u32[]{:S(2)}) collective-permute-start(bf16[1,1,1552,128]{3,2,1,0:T(8,128)(2,1)S(1)} %slice.46), channel_id=1, source_target_pairs={{0,4},{1,5},{2,6},{3,7},{4,8},{5,9},{6,10},{7,11},{8,12},{9,13},{1... | collective-permute-start | bytes 1191944 | tf_op jit(solution)/shard_map/ppermute | solution.py:220
  24.5 11.1 %collective-permute-start.11 = (bf16[1,1,1552,128]{3,2,1,0:T(8,128)(2,1)S(1)}, bf16[1,1,1552,128]{3,2,1,0:T(8,128)(2,1)S(1)}, u32[]{:S(2)}, u32[]{:S(2)}) collective-permute-start(bf16[1,1,1552,128]{3,2,1,0:T(8,128)(2,1)S(1)} %slice.47), channel_id=1, source_target_pairs={{0,12},{1,13},{2,14},{3,15},{4,0},{5,1},{6,2},{7,3},{8,4},{9,5},{1... | collective-permute-start | bytes 1191944 | tf_op jit(solution)/shard_map/ppermute | solution.py:220
  27.6 11.9 %collective-permute-start.2 = (bf16[1,1,1552,128]{3,2,1,0:T(8,128)(2,1)S(1)}, bf16[1,1,1552,128]{3,2,1,0:T(8,128)(2,1)S(1)}, u32[]{:S(2)}, u32[]{:S(2)}) collective-permute-start(bf16[1,1,1552,128]{3,2,1,0:T(8,128)(2,1)S(1)} %slice.41), channel_id=1, source_target_pairs={{0,1},{1,2},{2,3},{3,0},{4,5},{5,6},{6,7},{7,4},{8,9},{9,10},{10,1... | collective-permute-start | bytes 1191944 | tf_op jit(solution)/shard_map/ppermute | solution.py:220
  29.2 10.3 %collective-permute-start.3 = (bf16[1,1,1552,128]{3,2,1,0:T(8,128)(2,1)S(1)}, bf16[1,1,1552,128]{3,2,1,0:T(8,128)(2,1)S(1)}, u32[]{:S(2)}, u32[]{:S(2)}) collective-permute-start(bf16[1,1,1552,128]{3,2,1,0:T(8,128)(2,1)S(1)} %slice.42), channel_id=1, source_target_pairs={{0,3},{1,0},{2,1},{3,2},{4,7},{5,4},{6,5},{7,6},{8,11},{9,8},{10,9... | collective-permute-start | bytes 1191944 | tf_op jit(solution)/shard_map/ppermute | solution.py:220
  36.1 70.5 %collective-permute-start.12 = (bf16[4,2,1552,128]{3,2,1,0:T(8,128)(2,1)S(1)}, bf16[4,2,1552,128]{3,2,1,0:T(8,128)(2,1)S(1)}, u32[]{:S(2)}, u32[]{:S(2)}) collective-permute-start(bf16[4,2,1552,128]{3,2,1,0:T(8,128)(2,1)S(1)} %maximum_maximum_fusion.1.refs_3_), channel_id=1, source_target_pairs={{0,1},{1,2},{2,3},{3,0},{4,5},{5,6},{6,7},{7,4},{8,9},{9,10},{10,1... | collective-permute-start | bytes 9535496 | tf_op jit(solution)/shard_map/ppermute | solution.py:220
  37.6 70.6 %collective-permute-start.14 = (bf16[4,2,1552,128]{3,2,1,0:T(8,128)(2,1)S(1)}, bf16[4,2,1552,128]{3,2,1,0:T(8,128)(2,1)S(1)}, u32[]{:S(2)}, u32[]{:S(2)}) collective-permute-start(bf16[4,2,1552,128]{3,2,1,0:T(8,128)(2,1)S(1)} %maximum_maximum_fusion.1.refs_3_), channel_id=1, source_target_pairs={{0,3},{1,0},{2,1},{3,2},{4,7},{5,4},{6,5},{7,6},{8,11},{9,8},{10,9... | collective-permute-start | bytes 9535496 | tf_op jit(solution)/shard_map/ppermute | solution.py:220
  39.9 71.6 %copy-start.2 = (bf16[4,2,1552,128]{3,2,1,0:T(8,128)(2,1)}, bf16[4,2,1552,128]{3,2,1,0:T(8,128)(2,1)S(1)}, u32[]{:S(2)}) copy-start(bf16[4,2,1552,128]{3,2,1,0:T(8,128)(2,1)S(1)} %maximum_maximum_fusion.refs_0_) | copy-start | bytes 9535492
  40.0 71.5 %collective-permute-start.4 = (bf16[4,2,1552,128]{3,2,1,0:T(8,128)(2,1)S(1)}, bf16[4,2,1552,128]{3,2,1,0:T(8,128)(2,1)S(1)}, u32[]{:S(2)}, u32[]{:S(2)}) collective-permute-start(bf16[4,2,1552,128]{3,2,1,0:T(8,128)(2,1)S(1)} %maximum_maximum_fusion.refs_0_), channel_id=1, source_target_pairs={{0,4},{1,5},{2,6},{3,7},{4,8},{5,9},{6,10},{7,11},{8,12},{9,13},{1... | collective-permute-start | bytes 9535496 | tf_op jit(solution)/shard_map/ppermute | solution.py:220
  40.4 71.3 %collective-permute-start.6 = (bf16[4,2,1552,128]{3,2,1,0:T(8,128)(2,1)S(1)}, bf16[4,2,1552,128]{3,2,1,0:T(8,128)(2,1)S(1)}, u32[]{:S(2)}, u32[]{:S(2)}) collective-permute-start(bf16[4,2,1552,128]{3,2,1,0:T(8,128)(2,1)S(1)} %maximum_maximum_fusion.refs_0_), channel_id=1, source_target_pairs={{0,12},{1,13},{2,14},{3,15},{4,0},{5,1},{6,2},{7,3},{8,4},{9,5},{1... | collective-permute-start | bytes 9535496 | tf_op jit(solution)/shard_map/ppermute | solution.py:220
  108.0 35.7 %collective-permute-start.13 = (bf16[2,2,1552,128]{3,2,1,0:T(8,128)(2,1)}, bf16[2,2,1552,128]{3,2,1,0:T(8,128)(2,1)S(1)}, u32[]{:S(2)}, u32[]{:S(2)}) collective-permute-start(bf16[2,2,1552,128]{3,2,1,0:T(8,128)(2,1)} %slice.48), channel_id=1, source_target_pairs={{0,1},{1,2},{2,3},{3,0},{4,5},{5,6},{6,7},{7,4},{8,9},{9,10},{10,1... | collective-permute-start | bytes 4767752 | tf_op jit(solution)/shard_map/ppermute | solution.py:220
  108.3 6.8 %copy-start.7 = (f32[4,8192]{1,0:T(4,128)S(1)}, f32[4,8192]{1,0:T(4,128)}, u32[]{:S(2)}) copy-start(f32[4,8192]{1,0:T(4,128)} %param.5) | copy-start | bytes 393220
  108.3 35.4 %collective-permute-start.15 = (bf16[2,2,1552,128]{3,2,1,0:T(8,128)(2,1)S(1)}, bf16[2,2,1552,128]{3,2,1,0:T(8,128)(2,1)S(1)}, u32[]{:S(2)}, u32[]{:S(2)}) collective-permute-start(bf16[2,2,1552,128]{3,2,1,0:T(8,128)(2,1)S(1)} %slice.49), channel_id=1, source_target_pairs={{0,3},{1,0},{2,1},{3,2},{4,7},{5,4},{6,5},{7,6},{8,11},{9,8},{10,9... | collective-permute-start | bytes 4767752 | tf_op jit(solution)/shard_map/ppermute | solution.py:220
  111.6 35.0 %collective-permute-start.5 = (bf16[2,2,1552,128]{3,2,1,0:T(8,128)(2,1)S(1)}, bf16[2,2,1552,128]{3,2,1,0:T(8,128)(2,1)S(1)}, u32[]{:S(2)}, u32[]{:S(2)}) collective-permute-start(bf16[2,2,1552,128]{3,2,1,0:T(8,128)(2,1)S(1)} %slice.43), channel_id=1, source_target_pairs={{0,4},{1,5},{2,6},{3,7},{4,8},{5,9},{6,10},{7,11},{8,12},{9,13},{1... | collective-permute-start | bytes 4767752 | tf_op jit(solution)/shard_map/ppermute | solution.py:220
  111.8 34.7 %collective-permute-start.7 = (bf16[2,2,1552,128]{3,2,1,0:T(8,128)(2,1)S(1)}, bf16[2,2,1552,128]{3,2,1,0:T(8,128)(2,1)S(1)}, u32[]{:S(2)}, u32[]{:S(2)}) collective-permute-start(bf16[2,2,1552,128]{3,2,1,0:T(8,128)(2,1)S(1)} %slice.44), channel_id=1, source_target_pairs={{0,12},{1,13},{2,14},{3,15},{4,0},{5,1},{6,2},{7,3},{8,4},{9,5},{1... | collective-permute-start | bytes 4767752 | tf_op jit(solution)/shard_map/ppermute | solution.py:220
  149.4 2.1 collective-permute-start.17
  150.8 2.3 collective-permute-start.16
  152.3 2.1 collective-permute-start.19
  153.7 2.1 collective-permute-start.18
  155.1 2.1 collective-permute-start.21
  156.5 2.1 collective-permute-start.20
  157.9 2.1 collective-permute-start.23
  159.2 2.1 collective-permute-start.22
  160.6 2.1 collective-permute-start.25
  162.0 2.3 collective-permute-start.24
  163.6 2.1 collective-permute-start.27
  165.0 2.7 %collective-permute-start.26 = (bf16[64,32,128]{2,1,0:T(8,128)(2,1)S(1)}, bf16[64,32,128]{2,1,0:T(8,128)(2,1)S(1)}, u32[]{:S(2)}, u32[]{:S(2)}) collective-permute-start(bf16[64,32,128]{2,1,0:T(8,128)(2,1)S(1)} %get-tuple-element.89), channel_id=1, source_target_pairs={{32,16},{33,17},{34,18},{35,19},{36,20},{37,21},{38,22},{39,23},{4... | collective-permute-start | bytes 1572872 | tf_op jit(solution)/shard_map/ppermute | solution.py:284
  166.4 59.7 %collective-permute-start.29 = (bf16[64,32,128]{2,1,0:T(8,128)(2,1)S(1)}, bf16[64,32,128]{2,1,0:T(8,128)(2,1)S(1)}, u32[]{:S(2)}, u32[]{:S(2)}) collective-permute-start(bf16[64,32,128]{2,1,0:T(8,128)(2,1)S(1)} %get-tuple-element.96), channel_id=1, source_target_pairs={{16,0},{17,1},{18,2},{19,3},{20,4},{21,5},{22,6},{23,7},{24,8},{25... | collective-permute-start | bytes 1572872 | tf_op jit(solution)/shard_map/ppermute | solution.py:284
  168.3 64.7 %collective-permute-start.28 = (bf16[64,32,128]{2,1,0:T(8,128)(2,1)S(1)}, bf16[64,32,128]{2,1,0:T(8,128)(2,1)S(1)}, u32[]{:S(2)}, u32[]{:S(2)}) collective-permute-start(bf16[64,32,128]{2,1,0:T(8,128)(2,1)S(1)} %get-tuple-element.95), channel_id=1, source_target_pairs={{16,0},{17,1},{18,2},{19,3},{20,4},{21,5},{22,6},{23,7},{24,8},{25... | collective-permute-start | bytes 1572872 | tf_op jit(solution)/shard_map/ppermute | solution.py:284
  (6 other events, 21.7 us)

commit v2 on v1

--- a/solution.py
+++ b/solution.py
@@ -155,8 +155,13 @@
     return out, front, results.pop(0) if results else None
 
 
-def assemble_kernel(places, *refs):
+def assemble_kernel(places, carries, *refs):
     count = len(places)
+    refs = list(refs)
+    carried = []
+    if carries:
+        carried.append(pltpu.make_async_copy(refs.pop(count), refs.pop(count + 2), refs[-1].at[count, 0]))
+        carried[0].start()
     sems, pads = refs[-1], refs[-1 - count : -1]
     pieces, earlier, (target, table) = refs[:count], refs[count : -3 - count], refs[-3 - count : -1 - count]
     steps, span, size = target.shape[1:]
@@ -187,30 +192,31 @@
             entries = jnp.sum(buffer[b, t].astype(jnp.float32), axis=0, keepdims=True)
             value = value + (pltpu.roll(entries, j * ENTRY, 1) if j else entries)
         table[pl.ds(skip + line, 1)] = value.astype(jnp.int32)
-    for copy in copies[1::2]:
+    for copy in copies[1::2] + carried:
         copy.wait()
 
 
-def assemble(pieces, places, blocks, steps, earlier=()):
+def assemble(pieces, places, blocks, steps, earlier=(), carry=()):
     anywhere = pl.BlockSpec(memory_space=pl.ANY)
     span, size = pieces[0].shape[2:]
     bytes_moved = sum(p.size * 4 for p in pieces)
     lines = blocks * steps * ENTRY // size + sum(e.shape[0] for e in earlier)
     vmem = pl.BlockSpec(memory_space=pltpu.VMEM)
     return pl.pallas_call(
-        functools.partial(assemble_kernel, places),
+        functools.partial(assemble_kernel, places, len(carry)),
         out_shape=(
             jax.ShapeDtypeStruct((blocks, steps, span, size), jnp.bfloat16),
             jax.ShapeDtypeStruct((lines, size), jnp.int32),
+            *[jax.ShapeDtypeStruct(c.shape, c.dtype) for c in carry],
         ),
-        in_specs=[anywhere] * len(pieces) + [vmem] * len(earlier),
-        out_specs=(anywhere, vmem),
+        in_specs=[anywhere] * (len(pieces) + len(carry)) + [vmem] * len(earlier),
+        out_specs=(anywhere, vmem, *[anywhere] * len(carry)),
         scratch_shapes=[pltpu.VMEM((*p.shape[:2], PAD, size), p.dtype) for p in pieces]
-        + [pltpu.SemaphoreType.DMA((len(pieces), 2))],
+        + [pltpu.SemaphoreType.DMA((len(pieces) + 1, 2))],
         compiler_params=pltpu.CompilerParams(vmem_limit_bytes=2 << 20),
         cost_estimate=pl.CostEstimate(flops=0, bytes_accessed=bytes_moved, transcendentals=0),
         name="assemble",
-    )(*pieces, *earlier)
+    )(*pieces, *carry, *earlier)
 
 
 def moved(value, dx, dy):
@@ -239,6 +245,43 @@
     return (bundle, below, above), (far_below, far_above)
 
 
+def prepare_kernel(columns, spot, source, late, early, tiles, sems):
+    steps, local_rows, kt, size = tiles.shape[:4]
+    half = steps // 2
+    copies = [pltpu.make_async_copy(source.at[s], tiles.at[s], sems.at[s]) for s in range(steps)]
+    for copy in reversed(copies):
+        copy.start()
+    lane = lax.broadcasted_iota(jnp.int32, (PAD, size), 1)
+    first = lax.broadcasted_iota(jnp.int32, (PAD, size), 0) == 0
+    for s in reversed(range(steps)):
+        target, t = (late, s - half) if s >= half else (early, s)
+        entries = [columns[s, r, k] for r in range(local_rows) for k in range(kt)] + [spot[0], spot[1]]
+        value = jnp.zeros((PAD, size), jnp.int32)
+        for i, entry in enumerate(entries):
+            value = jnp.where(first & (lane == i), entry, value)
+        copies[s].wait()
+        for r in range(local_rows):
+            for k in range(kt):
+                target[0, t, pl.ds((r * kt + k) * size, size)] = tiles[s, r, k].T
+        target[0, t, pl.ds(local_rows * kt * size, PAD)] = value.astype(jnp.float32).astype(jnp.bfloat16)
+
+
+def prepare(tiles, columns, spot):
+    steps, local_rows, kt, size = tiles.shape[:4]
+    smem = pl.BlockSpec(memory_space=pltpu.SMEM)
+    vmem = pl.BlockSpec(memory_space=pltpu.VMEM)
+    shape = jax.ShapeDtypeStruct((1, steps // 2, local_rows * kt * size + PAD, size), jnp.bfloat16)
+    return pl.pallas_call(
+        prepare_kernel,
+        out_shape=(shape, shape),
+        in_specs=[smem, smem, pl.BlockSpec(memory_space=pl.ANY)],
+        out_specs=(vmem, vmem),
+        scratch_shapes=[pltpu.VMEM(tiles.shape, tiles.dtype), pltpu.SemaphoreType.DMA((steps,))],
+        compiler_params=pltpu.CompilerParams(vmem_limit_bytes=16 << 20),
+        name="prepare",
+    )(columns, spot, pltpu.with_memory_space_constraint(tiles, pltpu.HBM))
+
+
 def on_device(noise, scale, tiles, columns):
     steps, local_samples, node_count = noise.shape
     local_rows, kt, size = tiles.shape[1:4]
@@ -248,20 +291,15 @@
     scale_rows = scale.reshape(steps, 1, node_count)
 
     span = local_rows * kt * size + PAD
-    turned = jnp.swapaxes(tiles, 3, 4).reshape(steps, span - PAD, size)
-    entries = jnp.concatenate(
-        [columns.reshape(steps, local_rows * kt), jnp.broadcast_to(spot, (steps, 2))], axis=1
-    ).astype(jnp.bfloat16)
-    entries = jnp.pad(entries[:, None], ((0, 0), (0, PAD - 1), (0, size - entries.shape[1])))
-    block = jnp.concatenate([turned, entries], axis=1)[None]
-
-    late_near, late_far = ring_gather(block[:, half:], 0, 1)
-    early_near, early_far = ring_gather(block[:, :half], 1, 0)
-    near, near_table = assemble(
+    late, early = prepare(tiles, columns, spot)
+    late_near, late_far = ring_gather(late, 0, 1)
+    early_near, early_far = ring_gather(early, 1, 0)
+    near, near_table, noise = assemble(
         [pltpu.with_memory_space_constraint(p, pltpu.HBM) for p in (*late_near, *early_near)],
         [(i * SIDE, s) for s in (half, 0) for i in range(3)],
         3 * SIDE,
         steps,
+        carry=(noise,),
     )
     far, table = assemble(
         (*late_far, *early_far),

time: 240 us -> 239 us (level)
  Pallas kernels: 29.1 us -> 31.7 us
  local copies, waits for them, and re-layouts: 5.72 us -> 3.17 us
    pallas_call x2 -> x3, Pallas kernels: 7.34 us -> 9.98 us  [the longest x2 7.66 us: assemble(): pl.pallas_call(functools.partial(assemble_kernel, places, len(carry)), ou...]
where the time goes in v2:
time: 239 us; the launch traced here: 238 us
  waiting for transfers between devices  165 us (69%)
  starting transfers between devices  37 us (15%)
  Pallas kernels  31.7 us (13%)
  local copies, waits for them, and re-layouts  3.17 us (1%)
    ppermute x16, waiting for transfers between devices, moved(): return lax.ppermute(value, 'space', pairs)  107 us
    ppermute x14, waiting for transfers between devices, on_device(): fronts[block] = lax.ppermute(front, 'tm', [(part, part - 1)])  57.9 us
    ppermute x16, starting transfers between devices, moved(): return lax.ppermute(value, 'space', pairs)  26.1 us
    pallas_call x16, Pallas kernels, sweep(): pl.pallas_call(functools.partial(sweep_kernel, part, block, before, front...  21.7 us
    ppermute x14, starting transfers between devices, on_device(): fronts[block] = lax.ppermute(front, 'tm', [(part, part - 1)])  10.9 us
    pallas_call x2, Pallas kernels, assemble(): pl.pallas_call(functools.partial(assemble_kernel, places, len(carry)), ou...  7.66 us
  transfers between devices with their start and end apart: 30, of which 7 were waited for; matrix products, arithmetic and copies ran while one was open for 1% of the time, Pallas kernels for 9%

profile of v2, /device:TPU:0, one launch (start us, length us, event | category | flops | bytes accessed | tf_op | source)
XLA Modules:
  0.0 238.2 jit_solution(1440853889766610442)
XLA Ops:
  0.0 0.8 copy.20.columns
  0.9 2.3 prepare.1
  3.2 1.7 collective-permute-start.8
  4.9 1.6 collective-permute-start.9
  6.5 1.6 collective-permute-start
  8.1 1.7 collective-permute-start.1
  9.7 14.3 %collective-permute-done.8 = bf16[1,2,1552,128]{3,2,1,0:T(8,128)(2,1)S(1)} collective-permute-done((bf16[1,2,1552,128]{3,2,1,0:T(8,128)(2,1)S(1)}, bf16[1,2,1552,128]{3,2,1,0:T(8,128)(2,1)S(1)}, u32[]{:S(2)}, u32[]{:S(2)}) %collective-permute-start.8) | collective-permute-done | bytes 794656 | tf_op jit(solution)/shard_map/ppermute | solution.py:226
  24.5 3.0 %collective-permute-start.11 = (bf16[1,1,1552,128]{3,2,1,0:T(8,128)(2,1)S(1)}, bf16[1,1,1552,128]{3,2,1,0:T(8,128)(2,1)S(1)}, u32[]{:S(2)}, u32[]{:S(2)}) collective-permute-start(bf16[1,1,1552,128]{3,2,1,0:T(8,128)(2,1)S(1)} %slice.37), channel_id=1, source_target_pairs={{0,12},{1,13},{2,14},{3,15},{4,0},{5,1},{6,2},{7,3},{8,4},{9,5},{1... | collective-permute-start | bytes 1191944 | tf_op jit(solution)/shard_map/ppermute | solution.py:226
  27.6 1.6 collective-permute-start.2
  29.2 1.8 collective-permute-start.3
  31.0 4.7 %collective-permute-done.10 = bf16[1,1,1552,128]{3,2,1,0:T(8,128)(2,1)S(1)} collective-permute-done((bf16[1,1,1552,128]{3,2,1,0:T(8,128)(2,1)S(1)}, bf16[1,1,1552,128]{3,2,1,0:T(8,128)(2,1)S(1)}, u32[]{:S(2)}, u32[]{:S(2)}) %collective-permute-start.10) | collective-permute-done | bytes 397344 | tf_op jit(solution)/shard_map/ppermute | solution.py:226
  36.1 1.5 collective-permute-start.12
  37.6 1.8 collective-permute-start.14
  40.3 2.9 %collective-permute-start.6 = (bf16[4,2,1552,128]{3,2,1,0:T(8,128)(2,1)S(1)}, bf16[4,2,1552,128]{3,2,1,0:T(8,128)(2,1)S(1)}, u32[]{:S(2)}, u32[]{:S(2)}) collective-permute-start(bf16[4,2,1552,128]{3,2,1,0:T(8,128)(2,1)S(1)} %maximum_maximum_fusion.refs_0_), channel_id=1, source_target_pairs={{0,12},{1,13},{2,14},{3,15},{4,0},{5,1},{6,2},{7,3},{8,4},{9,5},{1... | collective-permute-start | bytes 9535496 | tf_op jit(solution)/shard_map/ppermute | solution.py:226
  43.2 63.4 %collective-permute-done.12.refs_4_ = bf16[4,2,1552,128]{3,2,1,0:T(8,128)(2,1)S(1)} collective-permute-done((bf16[4,2,1552,128]{3,2,1,0:T(8,128)(2,1)S(1)}, bf16[4,2,1552,128]{3,2,1,0:T(8,128)(2,1)S(1)}, u32[]{:S(2)}, u32[]{:S(2)}) %collective-permute-start.12) | collective-permute-done | bytes 3178528 | tf_op jit(solution)/shard_map/ppermute | solution.py:226
  106.6 1.4 slice.38
  108.8 2.7 %collective-permute-start.15 = (bf16[2,2,1552,128]{3,2,1,0:T(8,128)(2,1)S(1)}, bf16[2,2,1552,128]{3,2,1,0:T(8,128)(2,1)S(1)}, u32[]{:S(2)}, u32[]{:S(2)}) collective-permute-start(bf16[2,2,1552,128]{3,2,1,0:T(8,128)(2,1)S(1)} %slice.39), channel_id=1, source_target_pairs={{0,3},{1,0},{2,1},{3,2},{4,7},{5,4},{6,5},{7,6},{8,11},{9,8},{10,9... | collective-permute-start | bytes 4767752 | tf_op jit(solution)/shard_map/ppermute | solution.py:226
  111.8 3.3 %collective-permute-start.7 = (bf16[2,2,1552,128]{3,2,1,0:T(8,128)(2,1)S(1)}, bf16[2,2,1552,128]{3,2,1,0:T(8,128)(2,1)S(1)}, u32[]{:S(2)}, u32[]{:S(2)}) collective-permute-start(bf16[2,2,1552,128]{3,2,1,0:T(8,128)(2,1)S(1)} %slice.35), channel_id=1, source_target_pairs={{0,12},{1,13},{2,14},{3,15},{4,0},{5,1},{6,2},{7,3},{8,4},{9,5},{1... | collective-permute-start | bytes 4767752 | tf_op jit(solution)/shard_map/ppermute | solution.py:226
  115.2 7.0 %assemble.2 = (bf16[12,4,1552,128]{3,2,1,0:T(8,128)(2,1)S(1)}, s32[6,128]{1,0:T(8,128)S(1)}, bf16[4,64,8192]{2,1,0:T(8,128)(2,1)S(1)}) custom-call(bf16[4,2,1552,128]{3,2,1,0:T(8,128)(2,1)} %copy-done.2, bf16[4,2,1552,128]{3,2,1,0:T(8,128)(2,1)} %copy-done.5, bf16[4,2,1552,128]{3,2,1,0:T(8,128)(2,1)} %copy-done.6, bf16[4,2,1552,128]{3,2,1,0:T(8,128)(2,1)} %copy-done.1, ...), custom_call_target="tpu_custom_call" | custom-call | bytes 38141952 | tf_op jit(solution)/shard_map/assemble/pallas_call | solution.py:205
  122.2 21.5 %collective-permute-done.13.refs_2_ = bf16[2,2,1552,128]{3,2,1,0:T(8,128)(2,1)S(1)} collective-permute-done((bf16[2,2,1552,128]{3,2,1,0:T(8,128)(2,1)}, bf16[2,2,1552,128]{3,2,1,0:T(8,128)(2,1)S(1)}, u32[]{:S(2)}, u32[]{:S(2)}) %collective-permute-start.13) | collective-permute-done | bytes 1589280 | tf_op jit(solution)/shard_map/ppermute | solution.py:226
  143.7 2.9 %collective-permute-done.5.refs_0_ = bf16[2,2,1552,128]{3,2,1,0:T(8,128)(2,1)S(1)} collective-permute-done((bf16[2,2,1552,128]{3,2,1,0:T(8,128)(2,1)S(1)}, bf16[2,2,1552,128]{3,2,1,0:T(8,128)(2,1)S(1)}, u32[]{:S(2)}, u32[]{:S(2)}) %collective-permute-start.5) | collective-permute-done | bytes 1589280 | tf_op jit(solution)/shard_map/ppermute | solution.py:226
  149.3 0.7 collective-permute-start.16
  150.0 0.8 sweep.18
  153.6 0.7 collective-permute-start.21
  155.0 0.7 collective-permute-start.20
  161.2 0.9 sweep.26
  164.9 1.3 collective-permute-start.29
  166.8 1.3 collective-permute-start.28
  168.1 56.4 %collective-permute-done.29.refs_5_ = bf16[64,32,128]{2,1,0:T(8,128)(2,1)S(1)} collective-permute-done((bf16[64,32,128]{2,1,0:T(8,128)(2,1)S(1)}, bf16[64,32,128]{2,1,0:T(8,128)(2,1)S(1)}, u32[]{:S(2)}, u32[]{:S(2)}) %collective-permute-start.29) | collective-permute-done | bytes 524320 | tf_op jit(solution)/shard_map/ppermute | solution.py:322
  224.6 5.7 %sweep.30 = (bf16[4,64,8192]{2,1,0:T(8,128)(2,1)}, bf16[32,8192]{1,0:T(8,128)(2,1)S(1)}) custom-call(s32[1024]{0:T(1024)S(1)} %bitcast.17, bf16[12,4,1552,128]{3,2,1,0:T(8,128)(2,1)S(1)} %get-tuple-element.60.refs_1_, bf16[4,4,1552,128]{3,2,1,0:T(8,128)(2,1)S(1)} %get-tuple-element.61.refs_2_, ...), custom_call_target="tpu_custom_call", output_to_operand_aliasing={{0}: (7, {})} | custom-call | tf_op jit(solution)/shard_map/sweep/pallas_call | solution.py:136
  230.3 1.4 collective-permute-done.28.refs_5_
  231.6 6.4 %sweep.31 = bf16[4,64,8192]{2,1,0:T(8,128)(2,1)} custom-call(s32[1024]{0:T(1024)S(1)} %bitcast.18, bf16[12,4,1552,128]{3,2,1,0:T(8,128)(2,1)S(1)} %get-tuple-element.60.refs_1_, bf16[4,4,1552,128]{3,2,1,0:T(8,128)(2,1)S(1)} %get-tuple-element.61.refs_2_, bf16[4,64,8192]{2,1,0:T(8,128)(2,1)S(1)} %get-tuple-element.62.refs_3_, ...), custom_call_target="tpu_custom_call", output_to_operand_aliasing={{}: (7, {})} | custom-call | tf_op jit(solution)/shard_map/sweep/pallas_call | solution.py:136
  (76 shorter events, 18.0 us)
Async XLA Ops:
  3.2 20.9 %collective-permute-start.8 = (bf16[1,2,1552,128]{3,2,1,0:T(8,128)(2,1)S(1)}, bf16[1,2,1552,128]{3,2,1,0:T(8,128)(2,1)S(1)}, u32[]{:S(2)}, u32[]{:S(2)}) collective-permute-start(bf16[1,2,1552,128]{3,2,1,0:T(8,128)(2,1)S(1)} %get-tuple-element.57), channel_id=1, source_target_pairs={{0,4},{1,5},{2,6},{3,7},{4,8},{5,9},{6,10},{7,11},{8,12},{9,13},{1... | collective-permute-start | bytes 2383880 | tf_op jit(solution)/shard_map/ppermute | solution.py:226
  4.9 19.6 %collective-permute-start.9 = (bf16[1,2,1552,128]{3,2,1,0:T(8,128)(2,1)S(1)}, bf16[1,2,1552,128]{3,2,1,0:T(8,128)(2,1)S(1)}, u32[]{:S(2)}, u32[]{:S(2)}) collective-permute-start(bf16[1,2,1552,128]{3,2,1,0:T(8,128)(2,1)S(1)} %get-tuple-element.57), channel_id=1, source_target_pairs={{0,12},{1,13},{2,14},{3,15},{4,0},{5,1},{6,2},{7,3},{8,4},{9,5},{1... | collective-permute-start | bytes 2383880 | tf_op jit(solution)/shard_map/ppermute | solution.py:226
  6.5 21.0 %collective-permute-start = (bf16[1,2,1552,128]{3,2,1,0:T(8,128)(2,1)S(1)}, bf16[1,2,1552,128]{3,2,1,0:T(8,128)(2,1)S(1)}, u32[]{:S(2)}, u32[]{:S(2)}) collective-permute-start(bf16[1,2,1552,128]{3,2,1,0:T(8,128)(2,1)S(1)} %get-tuple-element.56), channel_id=1, source_target_pairs={{0,1},{1,2},{2,3},{3,0},{4,5},{5,6},{6,7},{7,4},{8,9},{9,10},{10,1... | collective-permute-start | bytes 2383880 | tf_op jit(solution)/shard_map/ppermute | solution.py:226
  8.1 21.0 %collective-permute-start.1 = (bf16[1,2,1552,128]{3,2,1,0:T(8,128)(2,1)S(1)}, bf16[1,2,1552,128]{3,2,1,0:T(8,128)(2,1)S(1)}, u32[]{:S(2)}, u32[]{:S(2)}) collective-permute-start(bf16[1,2,1552,128]{3,2,1,0:T(8,128)(2,1)S(1)} %get-tuple-element.56), channel_id=1, source_target_pairs={{0,3},{1,0},{2,1},{3,2},{4,7},{5,4},{6,5},{7,6},{8,11},{9,8},{10,9... | collective-permute-start | bytes 2383880 | tf_op jit(solution)/shard_map/ppermute | solution.py:226
  24.1 11.5 %collective-permute-start.10 = (bf16[1,1,1552,128]{3,2,1,0:T(8,128)(2,1)S(1)}, bf16[1,1,1552,128]{3,2,1,0:T(8,128)(2,1)S(1)}, u32[]{:S(2)}, u32[]{:S(2)}) collective-permute-start(bf16[1,1,1552,128]{3,2,1,0:T(8,128)(2,1)S(1)} %slice.36), channel_id=1, source_target_pairs={{0,4},{1,5},{2,6},{3,7},{4,8},{5,9},{6,10},{7,11},{8,12},{9,13},{1... | collective-permute-start | bytes 1191944 | tf_op jit(solution)/shard_map/ppermute | solution.py:226
  24.5 11.1 %collective-permute-start.11 = (bf16[1,1,1552,128]{3,2,1,0:T(8,128)(2,1)S(1)}, bf16[1,1,1552,128]{3,2,1,0:T(8,128)(2,1)S(1)}, u32[]{:S(2)}, u32[]{:S(2)}) collective-permute-start(bf16[1,1,1552,128]{3,2,1,0:T(8,128)(2,1)S(1)} %slice.37), channel_id=1, source_target_pairs={{0,12},{1,13},{2,14},{3,15},{4,0},{5,1},{6,2},{7,3},{8,4},{9,5},{1... | collective-permute-start | bytes 1191944 | tf_op jit(solution)/shard_map/ppermute | solution.py:226
  27.6 11.9 %collective-permute-start.2 = (bf16[1,1,1552,128]{3,2,1,0:T(8,128)(2,1)S(1)}, bf16[1,1,1552,128]{3,2,1,0:T(8,128)(2,1)S(1)}, u32[]{:S(2)}, u32[]{:S(2)}) collective-permute-start(bf16[1,1,1552,128]{3,2,1,0:T(8,128)(2,1)S(1)} %slice.32), channel_id=1, source_target_pairs={{0,1},{1,2},{2,3},{3,0},{4,5},{5,6},{6,7},{7,4},{8,9},{9,10},{10,1... | collective-permute-start | bytes 1191944 | tf_op jit(solution)/shard_map/ppermute | solution.py:226
  29.2 10.3 %collective-permute-start.3 = (bf16[1,1,1552,128]{3,2,1,0:T(8,128)(2,1)S(1)}, bf16[1,1,1552,128]{3,2,1,0:T(8,128)(2,1)S(1)}, u32[]{:S(2)}, u32[]{:S(2)}) collective-permute-start(bf16[1,1,1552,128]{3,2,1,0:T(8,128)(2,1)S(1)} %slice.33), channel_id=1, source_target_pairs={{0,3},{1,0},{2,1},{3,2},{4,7},{5,4},{6,5},{7,6},{8,11},{9,8},{10,9... | collective-permute-start | bytes 1191944 | tf_op jit(solution)/shard_map/ppermute | solution.py:226
  36.1 70.5 %collective-permute-start.12 = (bf16[4,2,1552,128]{3,2,1,0:T(8,128)(2,1)S(1)}, bf16[4,2,1552,128]{3,2,1,0:T(8,128)(2,1)S(1)}, u32[]{:S(2)}, u32[]{:S(2)}) collective-permute-start(bf16[4,2,1552,128]{3,2,1,0:T(8,128)(2,1)S(1)} %maximum_maximum_fusion.1.refs_3_), channel_id=1, source_target_pairs={{0,1},{1,2},{2,3},{3,0},{4,5},{5,6},{6,7},{7,4},{8,9},{9,10},{10,1... | collective-permute-start | bytes 9535496 | tf_op jit(solution)/shard_map/ppermute | solution.py:226
  37.6 70.6 %collective-permute-start.14 = (bf16[4,2,1552,128]{3,2,1,0:T(8,128)(2,1)S(1)}, bf16[4,2,1552,128]{3,2,1,0:T(8,128)(2,1)S(1)}, u32[]{:S(2)}, u32[]{:S(2)}) collective-permute-start(bf16[4,2,1552,128]{3,2,1,0:T(8,128)(2,1)S(1)} %maximum_maximum_fusion.1.refs_3_), channel_id=1, source_target_pairs={{0,3},{1,0},{2,1},{3,2},{4,7},{5,4},{6,5},{7,6},{8,11},{9,8},{10,9... | collective-permute-start | bytes 9535496 | tf_op jit(solution)/shard_map/ppermute | solution.py:226
  39.9 68.4 %copy-start.2 = (bf16[4,2,1552,128]{3,2,1,0:T(8,128)(2,1)}, bf16[4,2,1552,128]{3,2,1,0:T(8,128)(2,1)S(1)}, u32[]{:S(2)}) copy-start(bf16[4,2,1552,128]{3,2,1,0:T(8,128)(2,1)S(1)} %maximum_maximum_fusion.refs_0_) | copy-start | bytes 9535492
  39.9 71.5 %collective-permute-start.4 = (bf16[4,2,1552,128]{3,2,1,0:T(8,128)(2,1)S(1)}, bf16[4,2,1552,128]{3,2,1,0:T(8,128)(2,1)S(1)}, u32[]{:S(2)}, u32[]{:S(2)}) collective-permute-start(bf16[4,2,1552,128]{3,2,1,0:T(8,128)(2,1)S(1)} %maximum_maximum_fusion.refs_0_), channel_id=1, source_target_pairs={{0,4},{1,5},{2,6},{3,7},{4,8},{5,9},{6,10},{7,11},{8,12},{9,13},{1... | collective-permute-start | bytes 9535496 | tf_op jit(solution)/shard_map/ppermute | solution.py:226
  40.3 71.3 %collective-permute-start.6 = (bf16[4,2,1552,128]{3,2,1,0:T(8,128)(2,1)S(1)}, bf16[4,2,1552,128]{3,2,1,0:T(8,128)(2,1)S(1)}, u32[]{:S(2)}, u32[]{:S(2)}) collective-permute-start(bf16[4,2,1552,128]{3,2,1,0:T(8,128)(2,1)S(1)} %maximum_maximum_fusion.refs_0_), channel_id=1, source_target_pairs={{0,12},{1,13},{2,14},{3,15},{4,0},{5,1},{6,2},{7,3},{8,4},{9,5},{1... | collective-permute-start | bytes 9535496 | tf_op jit(solution)/shard_map/ppermute | solution.py:226
  108.0 35.7 %collective-permute-start.13 = (bf16[2,2,1552,128]{3,2,1,0:T(8,128)(2,1)}, bf16[2,2,1552,128]{3,2,1,0:T(8,128)(2,1)S(1)}, u32[]{:S(2)}, u32[]{:S(2)}) collective-permute-start(bf16[2,2,1552,128]{3,2,1,0:T(8,128)(2,1)} %slice.38), channel_id=1, source_target_pairs={{0,1},{1,2},{2,3},{3,0},{4,5},{5,6},{6,7},{7,4},{8,9},{9,10},{10,1... | collective-permute-start | bytes 4767752 | tf_op jit(solution)/shard_map/ppermute | solution.py:226
  108.8 6.4 %copy-start = (bf16[4,64,8192]{2,1,0:T(8,128)(2,1)S(1)}, bf16[4,64,8192]{2,1,0:T(8,128)(2,1)}, u32[]{:S(2)}) copy-start(bf16[4,64,8192]{2,1,0:T(8,128)(2,1)} %refs_6_.1) | copy-start | bytes 12582916
  108.8 34.9 %collective-permute-start.15 = (bf16[2,2,1552,128]{3,2,1,0:T(8,128)(2,1)S(1)}, bf16[2,2,1552,128]{3,2,1,0:T(8,128)(2,1)S(1)}, u32[]{:S(2)}, u32[]{:S(2)}) collective-permute-start(bf16[2,2,1552,128]{3,2,1,0:T(8,128)(2,1)S(1)} %slice.39), channel_id=1, source_target_pairs={{0,3},{1,0},{2,1},{3,2},{4,7},{5,4},{6,5},{7,6},{8,11},{9,8},{10,9... | collective-permute-start | bytes 4767752 | tf_op jit(solution)/shard_map/ppermute | solution.py:226
  111.6 35.0 %collective-permute-start.5 = (bf16[2,2,1552,128]{3,2,1,0:T(8,128)(2,1)S(1)}, bf16[2,2,1552,128]{3,2,1,0:T(8,128)(2,1)S(1)}, u32[]{:S(2)}, u32[]{:S(2)}) collective-permute-start(bf16[2,2,1552,128]{3,2,1,0:T(8,128)(2,1)S(1)} %slice.34), channel_id=1, source_target_pairs={{0,4},{1,5},{2,6},{3,7},{4,8},{5,9},{6,10},{7,11},{8,12},{9,13},{1... | collective-permute-start | bytes 4767752 | tf_op jit(solution)/shard_map/ppermute | solution.py:226
  111.8 34.7 %collective-permute-start.7 = (bf16[2,2,1552,128]{3,2,1,0:T(8,128)(2,1)S(1)}, bf16[2,2,1552,128]{3,2,1,0:T(8,128)(2,1)S(1)}, u32[]{:S(2)}, u32[]{:S(2)}) collective-permute-start(bf16[2,2,1552,128]{3,2,1,0:T(8,128)(2,1)S(1)} %slice.35), channel_id=1, source_target_pairs={{0,12},{1,13},{2,14},{3,15},{4,0},{5,1},{6,2},{7,3},{8,4},{9,5},{1... | collective-permute-start | bytes 4767752 | tf_op jit(solution)/shard_map/ppermute | solution.py:226
  147.9 2.1 collective-permute-start.17
  149.3 2.3 collective-permute-start.16
  150.8 2.1 collective-permute-start.19
  152.2 2.1 collective-permute-start.18
  153.6 2.1 collective-permute-start.21
  155.0 2.1 collective-permute-start.20
  156.4 2.1 collective-permute-start.23
  157.7 2.1 collective-permute-start.22
  159.1 2.1 collective-permute-start.25
  160.5 2.3 collective-permute-start.24
  162.1 2.1 collective-permute-start.27
  163.5 2.7 %collective-permute-start.26 = (bf16[64,32,128]{2,1,0:T(8,128)(2,1)S(1)}, bf16[64,32,128]{2,1,0:T(8,128)(2,1)S(1)}, u32[]{:S(2)}, u32[]{:S(2)}) collective-permute-start(bf16[64,32,128]{2,1,0:T(8,128)(2,1)S(1)} %get-tuple-element.95), channel_id=1, source_target_pairs={{32,16},{33,17},{34,18},{35,19},{36,20},{37,21},{38,22},{39,23},{4... | collective-permute-start | bytes 1572872 | tf_op jit(solution)/shard_map/ppermute | solution.py:322
  164.9 59.7 %collective-permute-start.29 = (bf16[64,32,128]{2,1,0:T(8,128)(2,1)S(1)}, bf16[64,32,128]{2,1,0:T(8,128)(2,1)S(1)}, u32[]{:S(2)}, u32[]{:S(2)}) collective-permute-start(bf16[64,32,128]{2,1,0:T(8,128)(2,1)S(1)} %get-tuple-element.102), channel_id=1, source_target_pairs={{16,0},{17,1},{18,2},{19,3},{20,4},{21,5},{22,6},{23,7},{24,8},{25... | collective-permute-start | bytes 1572872 | tf_op jit(solution)/shard_map/ppermute | solution.py:322
  166.8 64.8 %collective-permute-start.28 = (bf16[64,32,128]{2,1,0:T(8,128)(2,1)S(1)}, bf16[64,32,128]{2,1,0:T(8,128)(2,1)S(1)}, u32[]{:S(2)}, u32[]{:S(2)}) collective-permute-start(bf16[64,32,128]{2,1,0:T(8,128)(2,1)S(1)} %get-tuple-element.101), channel_id=1, source_target_pairs={{16,0},{17,1},{18,2},{19,3},{20,4},{21,5},{22,6},{23,7},{24,8},{25... | collective-permute-start | bytes 1572872 | tf_op jit(solution)/shard_map/ppermute | solution.py:322
  (6 other events, 22.9 us)

commit v3 on v2

--- a/solution.py
+++ b/solution.py
@@ -24,6 +24,7 @@
     if not (part == 0 and block == BLOCKS - 1):
         tail_out = refs.pop(0)
     out_buf, even, odd, out_sem, tail_sem = refs
+    odd = odd if front_out is None else front_out
     steps, size = near.shape[1], near.shape[3]
     depth = kt * size
     width = even.shape[1]
@@ -98,8 +99,6 @@
     def _active():
         even[...] = jnp.zeros(even.shape, even.dtype) if first else front[...]
         lax.fori_loop(0, steps, one_step, 0)
-        if front_out is not None:
-            front_out[...] = odd[...]
         if tail_out is None:
             out_copy(0).start()
             out_copy(0).wait()

time: 239 us -> 239 us (level)
  no operation moved by 1% of the time
where the time goes in v3:
time: 239 us
  waiting for transfers between devices  165 us (69%)
  starting transfers between devices  37 us (15%)
  Pallas kernels  31.7 us (13%)
  local copies, waits for them, and re-layouts  3.17 us (1%)
    ppermute x16, waiting for transfers between devices, moved(): return lax.ppermute(value, 'space', pairs)  107 us
    ppermute x14, waiting for transfers between devices, on_device(): fronts[block] = lax.ppermute(front, 'tm', [(part, part - 1)])  58.1 us
    ppermute x16, starting transfers between devices, moved(): return lax.ppermute(value, 'space', pairs)  26.1 us
    pallas_call x16, Pallas kernels, sweep(): pl.pallas_call(functools.partial(sweep_kernel, part, block, before, front...  21.7 us
    ppermute x14, starting transfers between devices, on_device(): fronts[block] = lax.ppermute(front, 'tm', [(part, part - 1)])  10.9 us
    pallas_call x2, Pallas kernels, assemble(): pl.pallas_call(functools.partial(assemble_kernel, places, len(carry)), ou...  7.66 us
  transfers between devices with their start and end apart: 30, of which 7 were waited for; matrix products, arithmetic and copies ran while one was open for 1% of the time, Pallas kernels for 9%

profile of v3, /device:TPU:0, one launch (start us, length us, event | category | flops | bytes accessed | tf_op | source)
XLA Modules:
  0.0 238.5 jit_solution(17533315069203539188)
XLA Ops:
  0.0 0.8 copy.20.columns
  0.9 2.3 prepare.1
  3.2 1.7 collective-permute-start.8
  4.9 1.6 collective-permute-start.9
  6.5 1.6 collective-permute-start
  8.1 1.7 collective-permute-start.1
  9.7 14.3 %collective-permute-done.8 = bf16[1,2,1552,128]{3,2,1,0:T(8,128)(2,1)S(1)} collective-permute-done((bf16[1,2,1552,128]{3,2,1,0:T(8,128)(2,1)S(1)}, bf16[1,2,1552,128]{3,2,1,0:T(8,128)(2,1)S(1)}, u32[]{:S(2)}, u32[]{:S(2)}) %collective-permute-start.8) | collective-permute-done | bytes 794656 | tf_op jit(solution)/shard_map/ppermute | solution.py:225
  24.5 3.0 %collective-permute-start.11 = (bf16[1,1,1552,128]{3,2,1,0:T(8,128)(2,1)S(1)}, bf16[1,1,1552,128]{3,2,1,0:T(8,128)(2,1)S(1)}, u32[]{:S(2)}, u32[]{:S(2)}) collective-permute-start(bf16[1,1,1552,128]{3,2,1,0:T(8,128)(2,1)S(1)} %slice.37), channel_id=1, source_target_pairs={{0,12},{1,13},{2,14},{3,15},{4,0},{5,1},{6,2},{7,3},{8,4},{9,5},{1... | collective-permute-start | bytes 1191944 | tf_op jit(solution)/shard_map/ppermute | solution.py:225
  27.6 1.6 collective-permute-start.2
  29.2 1.8 collective-permute-start.3
  31.0 4.7 %collective-permute-done.10 = bf16[1,1,1552,128]{3,2,1,0:T(8,128)(2,1)S(1)} collective-permute-done((bf16[1,1,1552,128]{3,2,1,0:T(8,128)(2,1)S(1)}, bf16[1,1,1552,128]{3,2,1,0:T(8,128)(2,1)S(1)}, u32[]{:S(2)}, u32[]{:S(2)}) %collective-permute-start.10) | collective-permute-done | bytes 397344 | tf_op jit(solution)/shard_map/ppermute | solution.py:225
  36.1 1.5 collective-permute-start.12
  37.6 1.8 collective-permute-start.14
  40.3 2.9 %collective-permute-start.6 = (bf16[4,2,1552,128]{3,2,1,0:T(8,128)(2,1)S(1)}, bf16[4,2,1552,128]{3,2,1,0:T(8,128)(2,1)S(1)}, u32[]{:S(2)}, u32[]{:S(2)}) collective-permute-start(bf16[4,2,1552,128]{3,2,1,0:T(8,128)(2,1)S(1)} %maximum_maximum_fusion.refs_0_), channel_id=1, source_target_pairs={{0,12},{1,13},{2,14},{3,15},{4,0},{5,1},{6,2},{7,3},{8,4},{9,5},{1... | collective-permute-start | bytes 9535496 | tf_op jit(solution)/shard_map/ppermute | solution.py:225
  43.2 63.4 %collective-permute-done.12.refs_4_ = bf16[4,2,1552,128]{3,2,1,0:T(8,128)(2,1)S(1)} collective-permute-done((bf16[4,2,1552,128]{3,2,1,0:T(8,128)(2,1)S(1)}, bf16[4,2,1552,128]{3,2,1,0:T(8,128)(2,1)S(1)}, u32[]{:S(2)}, u32[]{:S(2)}) %collective-permute-start.12) | collective-permute-done | bytes 3178528 | tf_op jit(solution)/shard_map/ppermute | solution.py:225
  106.6 1.4 slice.38
  108.8 2.7 %collective-permute-start.15 = (bf16[2,2,1552,128]{3,2,1,0:T(8,128)(2,1)S(1)}, bf16[2,2,1552,128]{3,2,1,0:T(8,128)(2,1)S(1)}, u32[]{:S(2)}, u32[]{:S(2)}) collective-permute-start(bf16[2,2,1552,128]{3,2,1,0:T(8,128)(2,1)S(1)} %slice.39), channel_id=1, source_target_pairs={{0,3},{1,0},{2,1},{3,2},{4,7},{5,4},{6,5},{7,6},{8,11},{9,8},{10,9... | collective-permute-start | bytes 4767752 | tf_op jit(solution)/shard_map/ppermute | solution.py:225
  111.8 3.3 %collective-permute-start.7 = (bf16[2,2,1552,128]{3,2,1,0:T(8,128)(2,1)S(1)}, bf16[2,2,1552,128]{3,2,1,0:T(8,128)(2,1)S(1)}, u32[]{:S(2)}, u32[]{:S(2)}) collective-permute-start(bf16[2,2,1552,128]{3,2,1,0:T(8,128)(2,1)S(1)} %slice.35), channel_id=1, source_target_pairs={{0,12},{1,13},{2,14},{3,15},{4,0},{5,1},{6,2},{7,3},{8,4},{9,5},{1... | collective-permute-start | bytes 4767752 | tf_op jit(solution)/shard_map/ppermute | solution.py:225
  115.2 7.0 %assemble.2 = (bf16[12,4,1552,128]{3,2,1,0:T(8,128)(2,1)S(1)}, s32[6,128]{1,0:T(8,128)S(1)}, bf16[4,64,8192]{2,1,0:T(8,128)(2,1)S(1)}) custom-call(bf16[4,2,1552,128]{3,2,1,0:T(8,128)(2,1)} %copy-done.2, bf16[4,2,1552,128]{3,2,1,0:T(8,128)(2,1)} %copy-done.5, bf16[4,2,1552,128]{3,2,1,0:T(8,128)(2,1)} %copy-done.6, bf16[4,2,1552,128]{3,2,1,0:T(8,128)(2,1)} %copy-done.1, ...), custom_call_target="tpu_custom_call" | custom-call | bytes 38141952 | tf_op jit(solution)/shard_map/assemble/pallas_call | solution.py:204
  122.2 21.5 %collective-permute-done.13.refs_2_ = bf16[2,2,1552,128]{3,2,1,0:T(8,128)(2,1)S(1)} collective-permute-done((bf16[2,2,1552,128]{3,2,1,0:T(8,128)(2,1)}, bf16[2,2,1552,128]{3,2,1,0:T(8,128)(2,1)S(1)}, u32[]{:S(2)}, u32[]{:S(2)}) %collective-permute-start.13) | collective-permute-done | bytes 1589280 | tf_op jit(solution)/shard_map/ppermute | solution.py:225
  143.7 2.9 %collective-permute-done.5.refs_0_ = bf16[2,2,1552,128]{3,2,1,0:T(8,128)(2,1)S(1)} collective-permute-done((bf16[2,2,1552,128]{3,2,1,0:T(8,128)(2,1)S(1)}, bf16[2,2,1552,128]{3,2,1,0:T(8,128)(2,1)S(1)}, u32[]{:S(2)}, u32[]{:S(2)}) %collective-permute-start.5) | collective-permute-done | bytes 1589280 | tf_op jit(solution)/shard_map/ppermute | solution.py:225
  150.0 0.8 sweep.18
  153.6 0.7 collective-permute-start.21
  155.0 0.7 collective-permute-start.20
  157.7 0.7 collective-permute-start.22
  161.2 0.9 sweep.26
  164.9 1.3 collective-permute-start.29
  166.8 1.3 collective-permute-start.28
  168.1 56.7 %collective-permute-done.29.refs_5_ = bf16[64,32,128]{2,1,0:T(8,128)(2,1)S(1)} collective-permute-done((bf16[64,32,128]{2,1,0:T(8,128)(2,1)S(1)}, bf16[64,32,128]{2,1,0:T(8,128)(2,1)S(1)}, u32[]{:S(2)}, u32[]{:S(2)}) %collective-permute-start.29) | collective-permute-done | bytes 524320 | tf_op jit(solution)/shard_map/ppermute | solution.py:321
  224.8 5.7 %sweep.30 = (bf16[4,64,8192]{2,1,0:T(8,128)(2,1)}, bf16[32,8192]{1,0:T(8,128)(2,1)S(1)}) custom-call(s32[1024]{0:T(1024)S(1)} %bitcast.17, bf16[12,4,1552,128]{3,2,1,0:T(8,128)(2,1)S(1)} %get-tuple-element.60.refs_1_, bf16[4,4,1552,128]{3,2,1,0:T(8,128)(2,1)S(1)} %get-tuple-element.61.refs_2_, ...), custom_call_target="tpu_custom_call", output_to_operand_aliasing={{0}: (7, {})} | custom-call | tf_op jit(solution)/shard_map/sweep/pallas_call | solution.py:135
  230.5 1.4 collective-permute-done.28.refs_5_
  231.9 6.4 %sweep.31 = bf16[4,64,8192]{2,1,0:T(8,128)(2,1)} custom-call(s32[1024]{0:T(1024)S(1)} %bitcast.18, bf16[12,4,1552,128]{3,2,1,0:T(8,128)(2,1)S(1)} %get-tuple-element.60.refs_1_, bf16[4,4,1552,128]{3,2,1,0:T(8,128)(2,1)S(1)} %get-tuple-element.61.refs_2_, bf16[4,64,8192]{2,1,0:T(8,128)(2,1)S(1)} %get-tuple-element.62.refs_3_, ...), custom_call_target="tpu_custom_call", output_to_operand_aliasing={{}: (7, {})} | custom-call | tf_op jit(solution)/shard_map/sweep/pallas_call | solution.py:135
  (76 shorter events, 18.0 us)
Async XLA Ops:
  3.2 20.9 %collective-permute-start.8 = (bf16[1,2,1552,128]{3,2,1,0:T(8,128)(2,1)S(1)}, bf16[1,2,1552,128]{3,2,1,0:T(8,128)(2,1)S(1)}, u32[]{:S(2)}, u32[]{:S(2)}) collective-permute-start(bf16[1,2,1552,128]{3,2,1,0:T(8,128)(2,1)S(1)} %get-tuple-element.57), channel_id=1, source_target_pairs={{0,4},{1,5},{2,6},{3,7},{4,8},{5,9},{6,10},{7,11},{8,12},{9,13},{1... | collective-permute-start | bytes 2383880 | tf_op jit(solution)/shard_map/ppermute | solution.py:225
  4.9 19.6 %collective-permute-start.9 = (bf16[1,2,1552,128]{3,2,1,0:T(8,128)(2,1)S(1)}, bf16[1,2,1552,128]{3,2,1,0:T(8,128)(2,1)S(1)}, u32[]{:S(2)}, u32[]{:S(2)}) collective-permute-start(bf16[1,2,1552,128]{3,2,1,0:T(8,128)(2,1)S(1)} %get-tuple-element.57), channel_id=1, source_target_pairs={{0,12},{1,13},{2,14},{3,15},{4,0},{5,1},{6,2},{7,3},{8,4},{9,5},{1... | collective-permute-start | bytes 2383880 | tf_op jit(solution)/shard_map/ppermute | solution.py:225
  6.5 21.0 %collective-permute-start = (bf16[1,2,1552,128]{3,2,1,0:T(8,128)(2,1)S(1)}, bf16[1,2,1552,128]{3,2,1,0:T(8,128)(2,1)S(1)}, u32[]{:S(2)}, u32[]{:S(2)}) collective-permute-start(bf16[1,2,1552,128]{3,2,1,0:T(8,128)(2,1)S(1)} %get-tuple-element.56), channel_id=1, source_target_pairs={{0,1},{1,2},{2,3},{3,0},{4,5},{5,6},{6,7},{7,4},{8,9},{9,10},{10,1... | collective-permute-start | bytes 2383880 | tf_op jit(solution)/shard_map/ppermute | solution.py:225
  8.1 21.0 %collective-permute-start.1 = (bf16[1,2,1552,128]{3,2,1,0:T(8,128)(2,1)S(1)}, bf16[1,2,1552,128]{3,2,1,0:T(8,128)(2,1)S(1)}, u32[]{:S(2)}, u32[]{:S(2)}) collective-permute-start(bf16[1,2,1552,128]{3,2,1,0:T(8,128)(2,1)S(1)} %get-tuple-element.56), channel_id=1, source_target_pairs={{0,3},{1,0},{2,1},{3,2},{4,7},{5,4},{6,5},{7,6},{8,11},{9,8},{10,9... | collective-permute-start | bytes 2383880 | tf_op jit(solution)/shard_map/ppermute | solution.py:225
  24.1 11.5 %collective-permute-start.10 = (bf16[1,1,1552,128]{3,2,1,0:T(8,128)(2,1)S(1)}, bf16[1,1,1552,128]{3,2,1,0:T(8,128)(2,1)S(1)}, u32[]{:S(2)}, u32[]{:S(2)}) collective-permute-start(bf16[1,1,1552,128]{3,2,1,0:T(8,128)(2,1)S(1)} %slice.36), channel_id=1, source_target_pairs={{0,4},{1,5},{2,6},{3,7},{4,8},{5,9},{6,10},{7,11},{8,12},{9,13},{1... | collective-permute-start | bytes 1191944 | tf_op jit(solution)/shard_map/ppermute | solution.py:225
  24.5 11.1 %collective-permute-start.11 = (bf16[1,1,1552,128]{3,2,1,0:T(8,128)(2,1)S(1)}, bf16[1,1,1552,128]{3,2,1,0:T(8,128)(2,1)S(1)}, u32[]{:S(2)}, u32[]{:S(2)}) collective-permute-start(bf16[1,1,1552,128]{3,2,1,0:T(8,128)(2,1)S(1)} %slice.37), channel_id=1, source_target_pairs={{0,12},{1,13},{2,14},{3,15},{4,0},{5,1},{6,2},{7,3},{8,4},{9,5},{1... | collective-permute-start | bytes 1191944 | tf_op jit(solution)/shard_map/ppermute | solution.py:225
  27.6 11.9 %collective-permute-start.2 = (bf16[1,1,1552,128]{3,2,1,0:T(8,128)(2,1)S(1)}, bf16[1,1,1552,128]{3,2,1,0:T(8,128)(2,1)S(1)}, u32[]{:S(2)}, u32[]{:S(2)}) collective-permute-start(bf16[1,1,1552,128]{3,2,1,0:T(8,128)(2,1)S(1)} %slice.32), channel_id=1, source_target_pairs={{0,1},{1,2},{2,3},{3,0},{4,5},{5,6},{6,7},{7,4},{8,9},{9,10},{10,1... | collective-permute-start | bytes 1191944 | tf_op jit(solution)/shard_map/ppermute | solution.py:225
  29.2 10.3 %collective-permute-start.3 = (bf16[1,1,1552,128]{3,2,1,0:T(8,128)(2,1)S(1)}, bf16[1,1,1552,128]{3,2,1,0:T(8,128)(2,1)S(1)}, u32[]{:S(2)}, u32[]{:S(2)}) collective-permute-start(bf16[1,1,1552,128]{3,2,1,0:T(8,128)(2,1)S(1)} %slice.33), channel_id=1, source_target_pairs={{0,3},{1,0},{2,1},{3,2},{4,7},{5,4},{6,5},{7,6},{8,11},{9,8},{10,9... | collective-permute-start | bytes 1191944 | tf_op jit(solution)/shard_map/ppermute | solution.py:225
  36.1 70.5 %collective-permute-start.12 = (bf16[4,2,1552,128]{3,2,1,0:T(8,128)(2,1)S(1)}, bf16[4,2,1552,128]{3,2,1,0:T(8,128)(2,1)S(1)}, u32[]{:S(2)}, u32[]{:S(2)}) collective-permute-start(bf16[4,2,1552,128]{3,2,1,0:T(8,128)(2,1)S(1)} %maximum_maximum_fusion.1.refs_3_), channel_id=1, source_target_pairs={{0,1},{1,2},{2,3},{3,0},{4,5},{5,6},{6,7},{7,4},{8,9},{9,10},{10,1... | collective-permute-start | bytes 9535496 | tf_op jit(solution)/shard_map/ppermute | solution.py:225
  37.6 70.6 %collective-permute-start.14 = (bf16[4,2,1552,128]{3,2,1,0:T(8,128)(2,1)S(1)}, bf16[4,2,1552,128]{3,2,1,0:T(8,128)(2,1)S(1)}, u32[]{:S(2)}, u32[]{:S(2)}) collective-permute-start(bf16[4,2,1552,128]{3,2,1,0:T(8,128)(2,1)S(1)} %maximum_maximum_fusion.1.refs_3_), channel_id=1, source_target_pairs={{0,3},{1,0},{2,1},{3,2},{4,7},{5,4},{6,5},{7,6},{8,11},{9,8},{10,9... | collective-permute-start | bytes 9535496 | tf_op jit(solution)/shard_map/ppermute | solution.py:225
  39.9 68.4 %copy-start.2 = (bf16[4,2,1552,128]{3,2,1,0:T(8,128)(2,1)}, bf16[4,2,1552,128]{3,2,1,0:T(8,128)(2,1)S(1)}, u32[]{:S(2)}) copy-start(bf16[4,2,1552,128]{3,2,1,0:T(8,128)(2,1)S(1)} %maximum_maximum_fusion.refs_0_) | copy-start | bytes 9535492
  39.9 71.5 %collective-permute-start.4 = (bf16[4,2,1552,128]{3,2,1,0:T(8,128)(2,1)S(1)}, bf16[4,2,1552,128]{3,2,1,0:T(8,128)(2,1)S(1)}, u32[]{:S(2)}, u32[]{:S(2)}) collective-permute-start(bf16[4,2,1552,128]{3,2,1,0:T(8,128)(2,1)S(1)} %maximum_maximum_fusion.refs_0_), channel_id=1, source_target_pairs={{0,4},{1,5},{2,6},{3,7},{4,8},{5,9},{6,10},{7,11},{8,12},{9,13},{1... | collective-permute-start | bytes 9535496 | tf_op jit(solution)/shard_map/ppermute | solution.py:225
  40.3 71.3 %collective-permute-start.6 = (bf16[4,2,1552,128]{3,2,1,0:T(8,128)(2,1)S(1)}, bf16[4,2,1552,128]{3,2,1,0:T(8,128)(2,1)S(1)}, u32[]{:S(2)}, u32[]{:S(2)}) collective-permute-start(bf16[4,2,1552,128]{3,2,1,0:T(8,128)(2,1)S(1)} %maximum_maximum_fusion.refs_0_), channel_id=1, source_target_pairs={{0,12},{1,13},{2,14},{3,15},{4,0},{5,1},{6,2},{7,3},{8,4},{9,5},{1... | collective-permute-start | bytes 9535496 | tf_op jit(solution)/shard_map/ppermute | solution.py:225
  108.0 35.7 %collective-permute-start.13 = (bf16[2,2,1552,128]{3,2,1,0:T(8,128)(2,1)}, bf16[2,2,1552,128]{3,2,1,0:T(8,128)(2,1)S(1)}, u32[]{:S(2)}, u32[]{:S(2)}) collective-permute-start(bf16[2,2,1552,128]{3,2,1,0:T(8,128)(2,1)} %slice.38), channel_id=1, source_target_pairs={{0,1},{1,2},{2,3},{3,0},{4,5},{5,6},{6,7},{7,4},{8,9},{9,10},{10,1... | collective-permute-start | bytes 4767752 | tf_op jit(solution)/shard_map/ppermute | solution.py:225
  108.8 6.4 %copy-start = (bf16[4,64,8192]{2,1,0:T(8,128)(2,1)S(1)}, bf16[4,64,8192]{2,1,0:T(8,128)(2,1)}, u32[]{:S(2)}) copy-start(bf16[4,64,8192]{2,1,0:T(8,128)(2,1)} %refs_6_.1) | copy-start | bytes 12582916
  108.8 34.9 %collective-permute-start.15 = (bf16[2,2,1552,128]{3,2,1,0:T(8,128)(2,1)S(1)}, bf16[2,2,1552,128]{3,2,1,0:T(8,128)(2,1)S(1)}, u32[]{:S(2)}, u32[]{:S(2)}) collective-permute-start(bf16[2,2,1552,128]{3,2,1,0:T(8,128)(2,1)S(1)} %slice.39), channel_id=1, source_target_pairs={{0,3},{1,0},{2,1},{3,2},{4,7},{5,4},{6,5},{7,6},{8,11},{9,8},{10,9... | collective-permute-start | bytes 4767752 | tf_op jit(solution)/shard_map/ppermute | solution.py:225
  111.6 35.0 %collective-permute-start.5 = (bf16[2,2,1552,128]{3,2,1,0:T(8,128)(2,1)S(1)}, bf16[2,2,1552,128]{3,2,1,0:T(8,128)(2,1)S(1)}, u32[]{:S(2)}, u32[]{:S(2)}) collective-permute-start(bf16[2,2,1552,128]{3,2,1,0:T(8,128)(2,1)S(1)} %slice.34), channel_id=1, source_target_pairs={{0,4},{1,5},{2,6},{3,7},{4,8},{5,9},{6,10},{7,11},{8,12},{9,13},{1... | collective-permute-start | bytes 4767752 | tf_op jit(solution)/shard_map/ppermute | solution.py:225
  111.8 34.7 %collective-permute-start.7 = (bf16[2,2,1552,128]{3,2,1,0:T(8,128)(2,1)S(1)}, bf16[2,2,1552,128]{3,2,1,0:T(8,128)(2,1)S(1)}, u32[]{:S(2)}, u32[]{:S(2)}) collective-permute-start(bf16[2,2,1552,128]{3,2,1,0:T(8,128)(2,1)S(1)} %slice.35), channel_id=1, source_target_pairs={{0,12},{1,13},{2,14},{3,15},{4,0},{5,1},{6,2},{7,3},{8,4},{9,5},{1... | collective-permute-start | bytes 4767752 | tf_op jit(solution)/shard_map/ppermute | solution.py:225
  147.9 2.1 collective-permute-start.17
  149.3 2.3 collective-permute-start.16
  150.8 2.1 collective-permute-start.19
  152.2 2.1 collective-permute-start.18
  153.6 2.1 collective-permute-start.21
  155.0 2.1 collective-permute-start.20
  156.3 2.1 collective-permute-start.23
  157.7 2.1 collective-permute-start.22
  159.1 2.1 collective-permute-start.25
  160.5 2.3 collective-permute-start.24
  162.1 2.1 collective-permute-start.27
  163.5 2.7 %collective-permute-start.26 = (bf16[64,32,128]{2,1,0:T(8,128)(2,1)S(1)}, bf16[64,32,128]{2,1,0:T(8,128)(2,1)S(1)}, u32[]{:S(2)}, u32[]{:S(2)}) collective-permute-start(bf16[64,32,128]{2,1,0:T(8,128)(2,1)S(1)} %get-tuple-element.95), channel_id=1, source_target_pairs={{32,16},{33,17},{34,18},{35,19},{36,20},{37,21},{38,22},{39,23},{4... | collective-permute-start | bytes 1572872 | tf_op jit(solution)/shard_map/ppermute | solution.py:321
  164.9 60.0 %collective-permute-start.29 = (bf16[64,32,128]{2,1,0:T(8,128)(2,1)S(1)}, bf16[64,32,128]{2,1,0:T(8,128)(2,1)S(1)}, u32[]{:S(2)}, u32[]{:S(2)}) collective-permute-start(bf16[64,32,128]{2,1,0:T(8,128)(2,1)S(1)} %get-tuple-element.102), channel_id=1, source_target_pairs={{16,0},{17,1},{18,2},{19,3},{20,4},{21,5},{22,6},{23,7},{24,8},{25... | collective-permute-start | bytes 1572872 | tf_op jit(solution)/shard_map/ppermute | solution.py:321
  166.8 65.1 %collective-permute-start.28 = (bf16[64,32,128]{2,1,0:T(8,128)(2,1)S(1)}, bf16[64,32,128]{2,1,0:T(8,128)(2,1)S(1)}, u32[]{:S(2)}, u32[]{:S(2)}) collective-permute-start(bf16[64,32,128]{2,1,0:T(8,128)(2,1)S(1)} %get-tuple-element.101), channel_id=1, source_target_pairs={{16,0},{17,1},{18,2},{19,3},{20,4},{21,5},{22,6},{23,7},{24,8},{25... | collective-permute-start | bytes 1572872 | tf_op jit(solution)/shard_map/ppermute | solution.py:321
  (6 other events, 22.9 us)
